TPU v7x, 512 devices: a whole 4x8x8 slice. The times are simulated.
512 devices in a mesh: slab: 32 (over y, x), sub: 16 (over z, core).
Axes of the slice: x: 4, y: 8, z: 8, core: 2. Of those that a mesh axis runs over, the one named last changes fastest.
Arguments:
- positions: float32 [3, 524288], P(None, 'slab'), may hold values from 0 to 129, as said below
- velocity: float32 [3, 524288], P(None, 'slab'), may hold values from -6 to 6
- density: float32 [524288], P('slab'), may hold values from 0.1 to 10
- pressure: float32 [524288], P('slab'), may hold values from 0.1 to 10
- counts: int32 [4096], P('slab'), may hold values from 8 to 128, as said below
- pair_list: int32 [3, 20480], P(None, ('slab', 'sub')), may hold values from -128 to 4095, as said below
Outputs:
- rates: float32 [5, 524288], P(None, 'slab')
Inputs may be any that keep to these rules, and one draw needn't show every extreme that they name: `positions`: particle k of leaf g lies in slab floor(g / 128) along x (x minus that index in [0, 1)), in column g mod 128 along y (likewise), and z in [0, 1). `counts`: at least 8 live particles a leaf; some leaf holds 128. `pair_list`: row 0 is a slot's home leaf, a leaf of this device's part of its slab (columns 8 * i to 8 * i + 7 on the device of index i along sub), or -1 for an empty slot. Row 1 is the other leaf, -1 for an empty slot: the home leaf itself, the leaf of the next column cyclically in the same slab, or a leaf of the next slab cyclically whose column is the home column - 1, + 0 or + 1 plus w, modulo 128; w is 0 for home leaves outside the last slab and one shift common to all pairs headed in the last slab. Row 2 is the image offset along y in units of cell width, 0 for an empty slot and for a pair of a leaf with itself; for a pair into the next slab, minus row 2 modulo 128 equals w. A leaf heads at most 5 pairs, each device holds at most 40 live slots, and some device holds exactly that many.
All inputs are finite; a program needn't handle non-finite values.
Results may differ from a plain program's by a relative error of at most 0.0003.
Values sent between devices are 32-bit elements; how exact they have to be, the bound alone decides.
A program may use at most 64 MiB of HBM per device.

v0:
```python
import math

import jax
import jax.numpy as jnp
from jax import lax
from jax.sharding import PartitionSpec as P

LEAF = 128
CAND = 5


GAMMA = 5.0 / 3.0
SUPPORT = 1.5
KERNEL_NORM = 21.0 / (2.0 * math.pi * SUPPORT**3)
MOMENT_REG = 0.05
SHEAR_SPEED = 1.0
AREA_FLOOR = 0.0001
SYM_PAIRS = ((0, 0), (0, 1), (0, 2), (1, 1), (1, 2), (2, 2))
UNIT_DIAG = (1.0, 0.0, 0.0, 1.0, 0.0, 1.0)


def shifted(shard, axis, by):
    peers = lax.axis_size(axis)
    return lax.ppermute(shard, axis, [(i, (i + by) % peers) for i in range(peers)])


def kernel(dist_sq):
    scaled = jnp.sqrt(dist_sq) / SUPPORT
    inside = jnp.maximum(1.0 - scaled, 0.0)
    return KERNEL_NORM * inside**4 * (1.0 + 4.0 * scaled)


def image_rows(tile, wrapped, offset, box_length):
    zero_row = jnp.zeros_like(offset)
    displace = jnp.stack(
        [
            wrapped * box_length,
            offset,
            zero_row,
            zero_row,
            -SHEAR_SPEED * wrapped,
            zero_row,
            zero_row,
            zero_row,
        ]
    )
    return tile + displace[:, :, None]


def sym_apply(matrix, vector):
    comp_x = matrix[0] * vector[0] + matrix[1] * vector[1] + matrix[2] * vector[2]
    comp_y = matrix[1] * vector[0] + matrix[3] * vector[1] + matrix[4] * vector[2]
    comp_z = matrix[2] * vector[0] + matrix[4] * vector[1] + matrix[5] * vector[2]
    return [comp_x, comp_y, comp_z]


def sym_inverse(matrix):
    entry_xx, entry_xy, entry_xz, entry_yy, entry_yz, entry_zz = matrix
    minor_xx = entry_yy * entry_zz - entry_yz * entry_yz
    minor_xy = entry_xz * entry_yz - entry_xy * entry_zz
    minor_xz = entry_xy * entry_yz - entry_xz * entry_yy
    minor_yy = entry_xx * entry_zz - entry_xz * entry_xz
    minor_yz = entry_xy * entry_xz - entry_xx * entry_yz
    minor_zz = entry_xx * entry_yy - entry_xy * entry_xy
    determinant = entry_xx * minor_xx + entry_xy * minor_xy + entry_xz * minor_xz
    return [
        minor / determinant
        for minor in (minor_xx, minor_xy, minor_xz, minor_yy, minor_yz, minor_zz)
    ]


def moment_tile(near_tile, far_tile, mask_near, mask_far, weight):
    separation = [
        far_tile[direction][:, None, :] - near_tile[direction][:, :, None] for direction in range(3)
    ]
    dist_sq = (
        separation[0] * separation[0]
        + separation[1] * separation[1]
        + separation[2] * separation[2]
    )
    smoothing = (
        kernel(dist_sq) * mask_near[:, :, None] * mask_far[:, None, :] * weight[:, None, None]
    )
    summands = [smoothing] + [
        smoothing * separation[left_axis] * separation[right_axis]
        for left_axis, right_axis in SYM_PAIRS
    ]
    for quantity in range(5):
        weighted = smoothing * (
            far_tile[3 + quantity][:, None, :] - near_tile[3 + quantity][:, :, None]
        )
        summands = summands + [weighted * separation[direction] for direction in range(3)]
    row_sums = jnp.stack([jnp.sum(summand, axis=2) for summand in summands])
    col_sums = jnp.stack([jnp.sum(summand, axis=1) for summand in summands])
    return (row_sums, col_sums)


def finish_moments(moments, live_mask):
    number_density = moments[0] + 1.0 - live_mask
    inverse_density = 1.0 / number_density
    second = [
        moments[1 + position] * inverse_density + MOMENT_REG * UNIT_DIAG[position]
        for position in range(6)
    ]
    inverse = sym_inverse(second)
    slopes = []
    for quantity in range(5):
        numerator = [
            moments[7 + 3 * quantity + direction] * inverse_density for direction in range(3)
        ]
        slopes = slopes + sym_apply(inverse, numerator)
    return jnp.stack([number_density] + inverse + slopes)


def side_flux(
    density_side, velocity_side, pressure_side, normal, normal_speed, lag_speed, wave_speed, contact
):
    energy = pressure_side / (GAMMA - 1.0) + 0.5 * density_side * (
        velocity_side[0] ** 2 + velocity_side[1] ** 2 + velocity_side[2] ** 2
    )
    plain_flux = [density_side * normal_speed]
    plain_flux = plain_flux + [
        density_side * velocity_side[direction] * normal_speed + pressure_side * normal[direction]
        for direction in range(3)
    ]
    plain_flux = plain_flux + [(energy + pressure_side) * normal_speed]
    conserved = (
        [density_side]
        + [density_side * velocity_side[direction] for direction in range(3)]
        + [energy]
    )
    factor = density_side * lag_speed / (wave_speed - contact)
    speed_gap = contact - normal_speed
    star_state = [factor] + [
        factor * (velocity_side[direction] + speed_gap * normal[direction])
        for direction in range(3)
    ]
    star_state = star_state + [
        factor
        * (
            energy / density_side
            + speed_gap * (contact + pressure_side / (density_side * lag_speed))
        )
    ]
    starred = [
        plain_flux[component] + wave_speed * (star_state[component] - conserved[component])
        for component in range(5)
    ]
    return (plain_flux, starred)


def hllc_flux(left_state, right_state, normal, face_vel):
    left_vel = [left_state[direction] - face_vel[direction] for direction in range(3)]
    right_vel = [right_state[direction] - face_vel[direction] for direction in range(3)]
    left_density, left_pressure = (left_state[3], left_state[4])
    right_density, right_pressure = (right_state[3], right_state[4])
    left_normal = left_vel[0] * normal[0] + left_vel[1] * normal[1] + left_vel[2] * normal[2]
    right_normal = right_vel[0] * normal[0] + right_vel[1] * normal[1] + right_vel[2] * normal[2]
    left_sound = jnp.sqrt(GAMMA * left_pressure / left_density)
    right_sound = jnp.sqrt(GAMMA * right_pressure / right_density)
    speed_left = jnp.minimum(left_normal - left_sound, right_normal - right_sound)
    speed_right = jnp.maximum(left_normal + left_sound, right_normal + right_sound)
    lag_left = speed_left - left_normal
    lag_right = speed_right - right_normal
    contact = (
        right_pressure
        - left_pressure
        + left_density * left_normal * lag_left
        - right_density * right_normal * lag_right
    ) / (left_density * lag_left - right_density * lag_right)
    flux_left, star_left = side_flux(
        left_density, left_vel, left_pressure, normal, left_normal, lag_left, speed_left, contact
    )
    flux_right, star_right = side_flux(
        right_density,
        right_vel,
        right_pressure,
        normal,
        right_normal,
        lag_right,
        speed_right,
        contact,
    )
    moving = [
        jnp.where(
            speed_left >= 0.0,
            flux_left[component],
            jnp.where(
                contact >= 0.0,
                star_left[component],
                jnp.where(speed_right >= 0.0, star_right[component], flux_right[component]),
            ),
        )
        for component in range(5)
    ]
    mass_flux = moving[0]
    momentum = [moving[1 + direction] + face_vel[direction] * mass_flux for direction in range(3)]
    face_sq = face_vel[0] ** 2 + face_vel[1] ** 2 + face_vel[2] ** 2
    energy_flux = (
        moving[4]
        + face_vel[0] * moving[1]
        + face_vel[1] * moving[2]
        + face_vel[2] * moving[3]
        + 0.5 * face_sq * mass_flux
    )
    return [mass_flux] + momentum + [energy_flux]


def flux_tile(near_tile, far_tile, near_pay, far_pay, mask_near, mask_far, weight):
    separation = [
        far_tile[direction][:, None, :] - near_tile[direction][:, :, None] for direction in range(3)
    ]
    dist_sq = (
        separation[0] * separation[0]
        + separation[1] * separation[1]
        + separation[2] * separation[2]
    )
    smoothing = kernel(dist_sq) * mask_near[:, :, None] * mask_far[:, None, :]
    near_density = near_pay[0][:, :, None]
    far_density = far_pay[0][:, None, :]
    near_matrix = [near_pay[1 + position][:, :, None] for position in range(6)]
    far_matrix = [far_pay[1 + position][:, None, :] for position in range(6)]
    toward_near = sym_apply(near_matrix, separation)
    toward_far = sym_apply(far_matrix, separation)
    near_scale = smoothing / (near_density * near_density)
    far_scale = smoothing / (far_density * far_density)
    area = [
        near_scale * toward_near[direction] + far_scale * toward_far[direction]
        for direction in range(3)
    ]
    magnitude = jnp.sqrt(area[0] * area[0] + area[1] * area[1] + area[2] * area[2])
    clamp_scale = 1.0 / jnp.maximum(magnitude, AREA_FLOOR)
    normal = [area[direction] * clamp_scale for direction in range(3)]
    left_state = []
    right_state = []
    for quantity in range(5):
        near_value = near_tile[3 + quantity][:, :, None]
        far_value = far_tile[3 + quantity][:, None, :]
        near_change = 0.5 * (
            near_pay[7 + 3 * quantity][:, :, None] * separation[0]
            + near_pay[8 + 3 * quantity][:, :, None] * separation[1]
            + near_pay[9 + 3 * quantity][:, :, None] * separation[2]
        )
        far_change = 0.5 * (
            far_pay[7 + 3 * quantity][:, None, :] * separation[0]
            + far_pay[8 + 3 * quantity][:, None, :] * separation[1]
            + far_pay[9 + 3 * quantity][:, None, :] * separation[2]
        )
        low_bound = jnp.minimum(near_value, far_value)
        high_bound = jnp.maximum(near_value, far_value)
        left_state.append(jnp.clip(near_value + near_change, low_bound, high_bound))
        right_state.append(jnp.clip(far_value - far_change, low_bound, high_bound))
    face_vel = [
        0.5 * (near_tile[3 + direction][:, :, None] + far_tile[3 + direction][:, None, :])
        for direction in range(3)
    ]
    fluxes = hllc_flux(left_state, right_state, normal, face_vel)
    pair_scale = magnitude * weight[:, None, None]
    row_sums = jnp.stack([-jnp.sum(pair_scale * face_flux, axis=2) for face_flux in fluxes])
    col_sums = jnp.stack([jnp.sum(pair_scale * face_flux, axis=1) for face_flux in fluxes])
    return (row_sums, col_sums)


def shards(positions, velocity, density, pressure, counts, pair_list):
    slab_leaves = counts.shape[0]
    slab_count = lax.axis_size("slab")
    slab_index = lax.axis_index("slab")
    state = jnp.concatenate([positions, velocity, density[None], pressure[None]], axis=0)
    upper_state, upper_counts = shifted((state, counts.astype(jnp.float32)), "slab", -1)
    slab_state = state.reshape(8, slab_leaves, LEAF)
    upper_slab = upper_state.reshape(8, slab_leaves, LEAF)
    upper_whole = upper_counts.astype(jnp.int32)
    box_length = jnp.asarray(slab_count, jnp.float32)
    slot_count = pair_list.shape[1]
    ranking = jnp.argsort((pair_list[0] < 0).astype(jnp.int32), stable=True)
    slots = pair_list[:, ranking]
    live_count = jnp.sum((pair_list[0] >= 0).astype(jnp.int32))
    occupied = slots[0] >= 0
    home_leaf = jnp.where(occupied, slots[0], 0)
    other_leaf = jnp.where(occupied, slots[1], 0)
    wrapped = (other_leaf // slab_leaves < home_leaf // slab_leaves).astype(jnp.float32)
    offset = slots[2].astype(jnp.float32)
    weight = jnp.where(occupied, jnp.where(home_leaf == other_leaf, 0.5, 1.0), 0.0).astype(
        jnp.float32
    )
    base_leaf = slab_index * slab_leaves
    turns = (live_count + CAND - 1) // CAND
    window = jnp.concatenate([slab_state, upper_slab], axis=1)
    window_counts = jnp.concatenate([counts, upper_whole])
    width = 2 * slab_leaves
    home_window = jnp.where(occupied, home_leaf - base_leaf, 0)
    other_window = jnp.where(occupied, (other_leaf - base_leaf) % (slab_count * slab_leaves), 0)
    window_mask = (jnp.arange(LEAF, dtype=jnp.int32)[None, :] < window_counts[:, None]).astype(
        jnp.float32
    )
    leaf_ids = jnp.arange(width, dtype=jnp.int32)
    home_hot = (home_window[:, None] == leaf_ids[None, :]).astype(jnp.float32)
    other_hot = (other_window[:, None] == leaf_ids[None, :]).astype(jnp.float32)

    def sweep(tile_fn, row_count):

        def one_turn(turn_index, buffers):
            row_buffer, col_buffer = buffers
            first_slot = turn_index * CAND
            home_part = lax.dynamic_slice_in_dim(home_window, first_slot, CAND)
            other_part = lax.dynamic_slice_in_dim(other_window, first_slot, CAND)
            wrap_part = lax.dynamic_slice_in_dim(wrapped, first_slot, CAND)
            offset_part = lax.dynamic_slice_in_dim(offset, first_slot, CAND)
            weight_part = lax.dynamic_slice_in_dim(weight, first_slot, CAND)
            row_sums, col_sums = tile_fn(home_part, other_part, wrap_part, offset_part, weight_part)
            row_buffer = lax.dynamic_update_slice_in_dim(row_buffer, row_sums, first_slot, 1)
            col_buffer = lax.dynamic_update_slice_in_dim(col_buffer, col_sums, first_slot, 1)
            return (row_buffer, col_buffer)

        empty = jnp.zeros((row_count, slot_count, LEAF), jnp.float32)
        row_buffer, col_buffer = lax.fori_loop(0, turns, one_turn, (empty, empty))
        total = jnp.einsum("rsp,sw->rwp", row_buffer, home_hot, precision=lax.Precision.HIGHEST)
        return total + jnp.einsum(
            "rsp,sw->rwp", col_buffer, other_hot, precision=lax.Precision.HIGHEST
        )

    def settle(partial_value):
        row_count = partial_value.shape[0]
        partial_value = lax.psum(partial_value, "sub")
        own_part = partial_value[:, :slab_leaves]
        next_part = partial_value[:, slab_leaves:]
        returned = shifted(next_part, "slab", 1)
        merged = own_part + returned
        return merged

    def moment_fn(home_part, other_part, wrap_part, offset_part, weight_part):
        near_tile = jnp.take(window, home_part, axis=1)
        far_tile = image_rows(
            jnp.take(window, other_part, axis=1), wrap_part, offset_part, box_length
        )
        return moment_tile(
            near_tile, far_tile, window_mask[home_part], window_mask[other_part], weight_part
        )

    moments = settle(sweep(moment_fn, 22))
    own_count = moments.shape[1]
    payload = finish_moments(moments, window_mask[:own_count])
    arrived = shifted(payload, "slab", -1)
    window_payload = jnp.concatenate([payload, arrived], axis=1)

    def flux_fn(home_part, other_part, wrap_part, offset_part, weight_part):
        near_tile = jnp.take(window, home_part, axis=1)
        far_tile = image_rows(
            jnp.take(window, other_part, axis=1), wrap_part, offset_part, box_length
        )
        near_pay = jnp.take(window_payload, home_part, axis=1)
        far_pay = jnp.take(window_payload, other_part, axis=1)
        return flux_tile(
            near_tile,
            far_tile,
            near_pay,
            far_pay,
            window_mask[home_part],
            window_mask[other_part],
            weight_part,
        )

    flux_sum = settle(sweep(flux_fn, 5))
    rate_part = (payload[0][None] * flux_sum).reshape(5, own_count * LEAF)
    return rate_part


def solution(mesh):
    placed = (
        P(None, "slab"),
        P(None, "slab"),
        P("slab"),
        P("slab"),
        P("slab"),
        P(None, ("slab", "sub")),
    )
    return jax.shard_map(
        shards, mesh=mesh, in_specs=placed, out_specs=P(None, "slab"), check_vma=False
    )
```

profile of v0, /device:TPU:1, one launch (start us, length us, event | category | flops | bytes accessed | tf_op | source)
XLA Modules:
  0.0 1030.3 jit_solution(6164458053880758125)
XLA Ops:
  7.3 8.1 collective-permute-start.1
  32.4 74.5 %while.30 = (s32[]{:T(128)}, f32[22,40,128]{2,1,0:T(8,128)S(1)}, f32[22,40,128]{2,1,0:T(8,128)S(1)}, s32[]{:T(128)}, s32[40]{0:T(128)}, /*index=5*/f32[8,256,128...) while((s32[]{:T(128)}, f32[22,40,128]{2,1,0:T(8,128)S(1)}, ...), condition=%wide.region_47.49_spmd.clone, body=%wide.region_2.48_spmd.clone.sunk | while | flops 9721420 | bytes 1241347 | solution.py:316
  112.9 125.7 %all-reduce.3.cloned.1.call-done = f32[22,256,128]{2,1,0:T(8,128)} async-done(((f32[22,256,128]{2,1,0:T(8,128)}), f32[22,256,128]{2,1,0:T(8,128)}) %all-reduce.3.cloned.1.call-update) | async-done | bytes 2883600 | tf_op jit(solution)/shard_map/psum | solution.py:324
  243.3 34.1 %collective-permute-done.2 = f32[22,128,128]{2,1,0:T(8,128)S(1)} collective-permute-done((f32[22,128,128]{2,1,0:T(8,128)S(1)}, f32[22,128,128]{2,1,0:T(8,128)S(1)}, u32[]{:S(2)}, u32[]{:S(2)}) %collective-permute-start.2) | collective-permute-done | bytes 1441824 | tf_op jit(solution)/shard_map/ppermute | solution.py:24
  282.0 29.6 %collective-permute-done.3 = f32[22,128,128]{2,1,0:T(8,128)S(1)} collective-permute-done((f32[22,128,128]{2,1,0:T(8,128)S(1)}, f32[22,128,128]{2,1,0:T(8,128)S(1)}, u32[]{:S(2)}, u32[]{:S(2)}) %collective-permute-start.3) | collective-permute-done | bytes 1441824 | tf_op jit(solution)/shard_map/ppermute | solution.py:24
  314.2 570.6 %while.31 = (s32[]{:T(128)}, f32[5,40,128]{2,1,0:T(8,128)}, f32[5,40,128]{2,1,0:T(8,128)S(1)}, s32[]{:T(128)}, s32[40]{0:T(128)}, /*index=5*/f32[8,256,128]{2,0,...) while((s32[]{:T(128)}, f32[5,40,128]{2,1,0:T(8,128)}, ...), condition=%wide.region_60.63_spmd.clone, body=%wide.region_49.62_spmd.clone.sunk | while | flops 113486544 | bytes 2761233 | solution.py:316
  364.9 6.3 fusion.255
  377.1 6.8 fusion.257
  436.2 6.3 fusion.255
  448.5 6.8 fusion.257
  507.5 6.3 fusion.255
  519.8 6.8 fusion.257
  578.9 6.3 fusion.255
  591.1 6.8 fusion.257
  650.2 6.3 fusion.255
  662.4 6.8 fusion.257
  721.5 6.3 fusion.255
  733.8 6.8 fusion.257
  792.8 6.3 fusion.255
  805.1 6.8 fusion.257
  864.1 6.3 fusion.255
  876.4 6.8 fusion.257
  888.3 118.4 %all-reduce.5.cloned.1.call-done = f32[5,256,128]{2,1,0:T(8,128)} async-done(((f32[5,256,128]{2,1,0:T(8,128)}), f32[5,256,128]{2,1,0:T(8,128)}) %all-reduce.5.cloned.1.call-update) | async-done | bytes 655376 | tf_op jit(solution)/shard_map/psum | solution.py:324
  1010.7 10.7 %collective-permute-done.4 = f32[5,128,128]{2,1,0:T(8,128)S(1)} collective-permute-done((f32[5,128,128]{2,1,0:T(8,128)S(1)}, f32[5,128,128]{2,1,0:T(8,128)S(1)}, u32[]{:S(2)}, u32[]{:S(2)}) %collective-permute-start.4) | collective-permute-done | bytes 327712 | tf_op jit(solution)/shard_map/ppermute | solution.py:24
  (2244 shorter events, 572.7 us)
Async XLA Ops:
  6.5 232.0 %all-reduce.3.cloned.1.call-start = ((), (), s32[]{:S(2)}) async-start(), calls=%async_computation | async-start | bytes 5767168 | tf_op jit(solution)/shard_map/psum | solution.py:324
  7.3 20.1 %collective-permute-start.1 = (f32[128]{0:T(128)S(1)}, f32[128]{0:T(128)S(1)}, u32[]{:S(2)}, u32[]{:S(2)}) collective-permute-start(f32[128]{0:T(128)S(1)} %convert_element_type.36), channel_id=1, source_target_pairs={{0,496},{16,0},{32,16},{48,32},{64,48},{80,64},{96,80},{112,96},{1... | collective-permute-start | bytes 1544 | tf_op jit(solution)/shard_map/ppermute | solution.py:24
  16.7 14.4 %collective-permute-start = (f32[8,16384]{1,0:T(8,128)S(1)}, f32[8,16384]{1,0:T(8,128)S(1)}, u32[]{:S(2)}, u32[]{:S(2)}) collective-permute-start(f32[8,16384]{1,0:T(8,128)S(1)} %pad_maximum_fusion.2), channel_id=1, source_target_pairs={{0,496},{16,0},{32,16},{48,32},{64,48},{80,64},{96,80},{112,96},{1... | collective-permute-start | bytes 1572872 | tf_op jit(solution)/shard_map/ppermute | solution.py:24
  112.8 893.8 %all-reduce.5.cloned.1.call-start = ((), (), s32[]{:S(2)}) async-start(), calls=%async_computation.1 | async-start | bytes 1310720 | tf_op jit(solution)/shard_map/psum | solution.py:324
  238.5 38.8 %copy-start = (f32[22,256,128]{2,1,0:T(8,128)S(1)}, f32[22,256,128]{2,1,0:T(8,128)}, u32[]{:S(2)}) copy-start(f32[22,256,128]{2,1,0:T(8,128)} %all-reduce.3.cloned.1.call-done) | copy-start | bytes 8650756
  240.1 37.2 %collective-permute-start.2 = (f32[22,128,128]{2,1,0:T(8,128)S(1)}, f32[22,128,128]{2,1,0:T(8,128)S(1)}, u32[]{:S(2)}, u32[]{:S(2)}) collective-permute-start(f32[22,128,128]{2,1,0:T(8,128)S(1)} %slice.766), channel_id=1, source_target_pairs={{0,16},{16,32},{32,48},{48,64},{64,80},{80,96},{96,112},{112,128},... | collective-permute-start | bytes 4325384 | tf_op jit(solution)/shard_map/ppermute | solution.py:24
  278.6 33.0 %collective-permute-start.3 = (f32[22,128,128]{2,1,0:T(8,128)S(1)}, f32[22,128,128]{2,1,0:T(8,128)S(1)}, u32[]{:S(2)}, u32[]{:S(2)}) collective-permute-start(f32[22,128,128]{2,1,0:T(8,128)S(1)} %bitcast_dynamic-update-slice_fusion), channel_id=1, source_target_pairs={{0,496},{16,0},{32,16},{48,32},{64,48},{80,64},{96,80},{112,96},{1... | collective-permute-start | bytes 4325384 | tf_op jit(solution)/shard_map/ppermute | solution.py:24
  330.0 28.8 %copy-start.6 = (f32[1,5,128]{2,1,0:T(8,128)S(1)}, f32[1,5,128]{2,1,0:T(8,128)}, u32[]{:S(2)}) copy-start(f32[1,5,128]{2,1,0:T(8,128)} %copy.379) | copy-start | bytes 7684 | tf_op jit(solution)/shard_map/while
  330.1 28.8 %copy-start.7 = (f32[1,5,128]{2,1,0:T(8,128)S(1)}, f32[1,5,128]{2,1,0:T(8,128)}, u32[]{:S(2)}) copy-start(f32[1,5,128]{2,1,0:T(8,128)} %copy.380) | copy-start | bytes 7684 | tf_op jit(solution)/shard_map/while
  330.1 28.8 %copy-start.8 = (f32[1,5,128]{2,1,0:T(8,128)S(1)}, f32[1,5,128]{2,1,0:T(8,128)}, u32[]{:S(2)}) copy-start(f32[1,5,128]{2,1,0:T(8,128)} %copy.381) | copy-start | bytes 7684 | tf_op jit(solution)/shard_map/while
  330.1 28.8 %copy-start.9 = (f32[1,5,128]{2,1,0:T(8,128)S(1)}, f32[1,5,128]{2,1,0:T(8,128)}, u32[]{:S(2)}) copy-start(f32[1,5,128]{2,1,0:T(8,128)} %copy.384) | copy-start | bytes 7684 | tf_op jit(solution)/shard_map/while
  330.1 28.8 %copy-start.10 = (f32[1,5,128]{2,1,0:T(8,128)S(1)}, f32[1,5,128]{2,1,0:T(8,128)}, u32[]{:S(2)}) copy-start(f32[1,5,128]{2,1,0:T(8,128)} %copy.385) | copy-start | bytes 7684 | tf_op jit(solution)/shard_map/while
  330.1 28.8 %copy-start.12 = (f32[1,5,128]{2,1,0:T(8,128)S(1)}, f32[1,5,128]{2,1,0:T(8,128)}, u32[]{:S(2)}) copy-start(f32[1,5,128]{2,1,0:T(8,128)} %copy.386) | copy-start | bytes 7684 | tf_op jit(solution)/shard_map/while
  343.9 33.2 %copy-start.11 = (f32[1,5,128]{2,1,0:T(8,128)S(1)}, f32[1,5,128]{2,1,0:T(8,128)}, u32[]{:S(2)}) copy-start(f32[1,5,128]{2,1,0:T(8,128)} %copy.385) | copy-start | bytes 7684 | tf_op jit(solution)/shard_map/while
  415.2 33.2 %copy-start.11 = (f32[1,5,128]{2,1,0:T(8,128)S(1)}, f32[1,5,128]{2,1,0:T(8,128)}, u32[]{:S(2)}) copy-start(f32[1,5,128]{2,1,0:T(8,128)} %copy.385) | copy-start | bytes 7684 | tf_op jit(solution)/shard_map/while
  472.7 28.8 %copy-start.6 = (f32[1,5,128]{2,1,0:T(8,128)S(1)}, f32[1,5,128]{2,1,0:T(8,128)}, u32[]{:S(2)}) copy-start(f32[1,5,128]{2,1,0:T(8,128)} %copy.379) | copy-start | bytes 7684 | tf_op jit(solution)/shard_map/while
  472.7 28.8 %copy-start.7 = (f32[1,5,128]{2,1,0:T(8,128)S(1)}, f32[1,5,128]{2,1,0:T(8,128)}, u32[]{:S(2)}) copy-start(f32[1,5,128]{2,1,0:T(8,128)} %copy.380) | copy-start | bytes 7684 | tf_op jit(solution)/shard_map/while
  486.5 33.2 %copy-start.11 = (f32[1,5,128]{2,1,0:T(8,128)S(1)}, f32[1,5,128]{2,1,0:T(8,128)}, u32[]{:S(2)}) copy-start(f32[1,5,128]{2,1,0:T(8,128)} %copy.385) | copy-start | bytes 7684 | tf_op jit(solution)/shard_map/while
  557.8 33.2 %copy-start.11 = (f32[1,5,128]{2,1,0:T(8,128)S(1)}, f32[1,5,128]{2,1,0:T(8,128)}, u32[]{:S(2)}) copy-start(f32[1,5,128]{2,1,0:T(8,128)} %copy.385) | copy-start | bytes 7684 | tf_op jit(solution)/shard_map/while
  629.2 33.2 %copy-start.11 = (f32[1,5,128]{2,1,0:T(8,128)S(1)}, f32[1,5,128]{2,1,0:T(8,128)}, u32[]{:S(2)}) copy-start(f32[1,5,128]{2,1,0:T(8,128)} %copy.385) | copy-start | bytes 7684 | tf_op jit(solution)/shard_map/while
  700.5 33.2 %copy-start.11 = (f32[1,5,128]{2,1,0:T(8,128)S(1)}, f32[1,5,128]{2,1,0:T(8,128)}, u32[]{:S(2)}) copy-start(f32[1,5,128]{2,1,0:T(8,128)} %copy.385) | copy-start | bytes 7684 | tf_op jit(solution)/shard_map/while
  771.8 33.2 %copy-start.11 = (f32[1,5,128]{2,1,0:T(8,128)S(1)}, f32[1,5,128]{2,1,0:T(8,128)}, u32[]{:S(2)}) copy-start(f32[1,5,128]{2,1,0:T(8,128)} %copy.385) | copy-start | bytes 7684 | tf_op jit(solution)/shard_map/while
  843.1 33.2 %copy-start.11 = (f32[1,5,128]{2,1,0:T(8,128)S(1)}, f32[1,5,128]{2,1,0:T(8,128)}, u32[]{:S(2)}) copy-start(f32[1,5,128]{2,1,0:T(8,128)} %copy.385) | copy-start | bytes 7684 | tf_op jit(solution)/shard_map/while
  1007.6 13.8 %collective-permute-start.4 = (f32[5,128,128]{2,1,0:T(8,128)S(1)}, f32[5,128,128]{2,1,0:T(8,128)S(1)}, u32[]{:S(2)}, u32[]{:S(2)}) collective-permute-start(f32[5,128,128]{2,1,0:T(8,128)S(1)} %slice.791), channel_id=1, source_target_pairs={{0,16},{16,32},{32,48},{48,64},{64,80},{80,96},{96,112},{112,128},... | collective-permute-start | bytes 983048 | tf_op jit(solution)/shard_map/ppermute | solution.py:24
  (324 other events, 6963.8 us)
Sparse Core Ops, SparseCore 0:
  112.9 125.5 all-reduce.2
  888.4 118.2 all-reduce.4
where the time goes:
time: 1030 us
  local copies, waits for them, and re-layouts  334 us (32%)
  waiting for transfers between devices  322 us (31%)
  other arithmetic  318 us (31%)
  starting transfers between devices  20.2 us (2%)
  between operations  14.4 us (1%)
  loops' own time  12.5 us (1%)
    reduce_sum x40, other arithmetic, flux_tile(): jnp.sum(pair_scale * face_flux, axis=1)  246 us
    psum x2, waiting for transfers between devices, settle(): partial_value = lax.psum(partial_value, 'sub')  244 us
    while x1648, local copies, waits for them, and re-layouts  234 us
    ppermute x5, waiting for transfers between devices, shifted(): lax.ppermute(shard, axis, [(i, (i + by) % peers) for i in range(peers)])  77.5 us
    reduce_sum x16, other arithmetic, moment_tile(): col_sums = jnp.stack([jnp.sum(summand, axis=1) for summand in summands])  29.6 us
  transfers between devices with their start and end apart: 7, of which 6 were waited for; matrix products, arithmetic and copies ran while one was open for 1% of the time, Pallas kernels for 0%

commit v1 on v0

v1 whole, which is shorter than its diff:
```python
import functools
import math

import jax
import jax.numpy as jnp
from jax import lax
from jax.experimental import pallas as pl
from jax.experimental.pallas import tpu as pltpu
from jax.sharding import PartitionSpec as P

LEAF = 128
KINDS = 5
WIN = 12
LEVELS = 4
GAMMA = 5.0 / 3.0
SUPPORT = 1.5
KERNEL_NORM = 21.0 / (2.0 * math.pi * SUPPORT**3)
MOMENT_REG = 0.05
AREA_FLOOR = 0.0001
FAR_AWAY = 1.0e6
DEAD_ABOVE = 1.0e5
TINY = 1.2e-38
BLOCK = 2
MESH = pl.DeviceIdType.MESH
VMEM = pl.BlockSpec(memory_space=pltpu.VMEM)
SMEM = pl.BlockSpec(memory_space=pltpu.SMEM)
HIGHEST = lax.Precision.HIGHEST


def around(value, size):
    return lax.rem(value + size, size)


def gather_kernel(slabs, subs, row_ref, out_ref, send_sem, recv_sem, own_sem):
    slab = lax.axis_index("slab")
    sub = lax.axis_index("sub")
    barrier = pltpu.get_barrier_semaphore()

    def greet(shift, first):
        def one(k, carry):
            pl.semaphore_signal(
                barrier,
                inc=1,
                device_id=(around(slab + shift, slabs), around(sub + k, subs)),
                device_id_type=MESH,
            )
            return carry

        lax.fori_loop(first, subs, one, 0)

    for shift in (-2, -1, 0, 1, 2):
        greet(shift, 1 if shift == 0 else 0)
    pl.semaphore_wait(barrier, 5 * subs - 1)

    own_slot = 2 * subs + sub
    own = pltpu.make_async_copy(row_ref, out_ref.at[pl.ds(own_slot, 1)], own_sem)
    own.start()

    def copy(shift, k):
        slot = (shift + 2) * subs + sub
        return pltpu.make_async_remote_copy(
            src_ref=row_ref,
            dst_ref=out_ref.at[pl.ds(slot, 1)],
            send_sem=send_sem.at[(shift + 2) * subs + k],
            recv_sem=recv_sem.at[slot],
            device_id=(around(slab - shift, slabs), around(sub + k, subs)),
            device_id_type=MESH,
        )

    def arrival(shift, k):
        slot = (shift + 2) * subs + around(sub + k, subs)
        return pltpu.make_async_remote_copy(
            src_ref=row_ref,
            dst_ref=out_ref.at[pl.ds(slot, 1)],
            send_sem=send_sem.at[(shift + 2) * subs + k],
            recv_sem=recv_sem.at[slot],
            device_id=(around(slab - shift, slabs), around(sub + k, subs)),
            device_id_type=MESH,
        )

    for shift in (-2, -1, 0, 1):
        first = 1 if shift == 0 else 0

        def send(k, carry, shift=shift):
            copy(shift, k).start()
            return carry

        lax.fori_loop(first, subs, send, 0)
    for shift in (-2, -1, 0, 1):
        first = 1 if shift == 0 else 0

        def settle(k, carry, shift=shift):
            copy(shift, k).wait_send()
            arrival(shift, k).wait_recv()
            return carry

        lax.fori_loop(first, subs, settle, 0)
    own.wait()


def gather_lists(row, slabs, subs):
    return pl.pallas_call(
        functools.partial(gather_kernel, slabs, subs),
        out_shape=jax.ShapeDtypeStruct((4 * subs, 1, LEAF), jnp.int32),
        in_specs=[VMEM],
        out_specs=VMEM,
        scratch_shapes=[
            pltpu.SemaphoreType.DMA((4 * subs,)),
            pltpu.SemaphoreType.DMA((4 * subs,)),
            pltpu.SemaphoreType.DMA,
        ],
        compiler_params=pltpu.CompilerParams(collective_id=0, has_side_effects=True),
        name="gather_lists",
    )(row)


def pair_tables(lists, slab, slabs, slots, slab_leaves):
    subs = lists.shape[0] // 4
    entries = lists.reshape(4, subs, LEAF)
    home = entries[:, :, :slots]
    other = entries[:, :, slots : 2 * slots]
    offset = entries[:, :, 2 * slots : 3 * slots]
    occupied = home >= 0
    home_slab = home // slab_leaves
    other_slab = other // slab_leaves
    crossing = occupied & (home_slab != other_slab)
    shear = jnp.max(
        jnp.where(crossing & (home_slab == slabs - 1), (-offset) % slab_leaves, 0)
    )
    step = (other % slab_leaves - home % slab_leaves + offset + 1) % slab_leaves
    kind = jnp.where(other == home, 0, jnp.where(crossing, 2 + step, 1))
    kind = jnp.where(kind < KINDS, kind, KINDS * slab_leaves)
    homes = slab_leaves // subs
    key = jnp.where(occupied, (home % homes) * KINDS + kind, -1)[1:]
    hot = key[:, :, None, :] == jnp.arange(homes * KINDS, dtype=jnp.int32)[:, None]
    number = jnp.sum(hot.astype(jnp.int32), axis=3)
    moved = jnp.max(jnp.where(hot, offset[1:][:, :, None, :], -(2**20)), axis=3)
    return shear, number.reshape(-1), moved.reshape(-1)


def window_kernel(
    slabs, subs, meta, counts, positions, velocity, density, pressure, own, below, above, beyond
):
    slab, sub, shear = meta[0], meta[1], meta[2]
    slab_leaves = counts.shape[0]
    homes = slab_leaves // subs
    no_shear = jnp.int32(0)
    shifts = (
        no_shear,
        jnp.where(slab == slabs - 1, -shear, no_shear),
        jnp.where(slab == 0, shear, no_shear),
        jnp.where(slab <= 1, shear, no_shear),
    )
    lane = lax.broadcasted_iota(jnp.int32, (1, LEAF), 1)
    row = lax.broadcasted_iota(jnp.int32, (3, LEAF), 0)
    for shift, target in zip(shifts, (own, below, above, beyond)):

        def one(slot, carry, shift=shift, target=target):
            column = lax.rem(sub * homes + slot - 2 + shift + 2 * slab_leaves, slab_leaves)
            start = pl.multiple_of(column * LEAF, LEAF)
            live = lane < counts[column]
            centre = jnp.where(
                row == 0,
                slab.astype(jnp.float32) + 0.5,
                jnp.where(row == 1, column.astype(jnp.float32) + 0.5, 0.5),
            )
            place = positions[:, pl.ds(start, LEAF)] - centre
            place = jnp.where((row > 0) | live, place, FAR_AWAY)
            target[slot, 0:3, :] = place
            target[slot, 3:6, :] = velocity[:, pl.ds(start, LEAF)]
            target[slot, 6:7, :] = density[pl.ds(column, 1), :]
            target[slot, 7:8, :] = pressure[pl.ds(column, 1), :]
            return carry

        lax.fori_loop(0, WIN, one, 0)


def leaf_windows(meta, counts, positions, velocity, density, pressure, slabs, subs):
    window = jax.ShapeDtypeStruct((WIN, 8, LEAF), jnp.float32)
    return pl.pallas_call(
        functools.partial(window_kernel, slabs, subs),
        out_shape=(window,) * 4,
        in_specs=[SMEM, SMEM, VMEM, VMEM, VMEM, VMEM],
        out_specs=(VMEM,) * 4,
        name="leaf_windows",
    )(meta, counts, positions, velocity, density, pressure)


def swap_kernel(
    slabs, below, above, beyond, got_below, got_above, got_beyond, send_sem, recv_sem
):
    slab = lax.axis_index("slab")
    sub = lax.axis_index("sub")
    barrier = pltpu.get_barrier_semaphore()
    for shift in (-2, -1, 1, 2):
        pl.semaphore_signal(
            barrier, inc=1, device_id=(around(slab + shift, slabs), sub), device_id_type=MESH
        )
    pl.semaphore_wait(barrier, 4)
    copies = []
    for k, (shift, source, target) in enumerate(
        ((1, below, got_below), (-1, above, got_above), (-2, beyond, got_beyond))
    ):
        copies.append(
            pltpu.make_async_remote_copy(
                src_ref=source,
                dst_ref=target,
                send_sem=send_sem.at[k],
                recv_sem=recv_sem.at[k],
                device_id=(around(slab + shift, slabs), sub),
                device_id_type=MESH,
            )
        )
        copies[-1].start()
    for one in copies:
        one.wait()


def swap_windows(below, above, beyond, slabs):
    window = jax.ShapeDtypeStruct((WIN, 8, LEAF), jnp.float32)
    return pl.pallas_call(
        functools.partial(swap_kernel, slabs),
        out_shape=(window,) * 3,
        in_specs=[VMEM] * 3,
        out_specs=(VMEM,) * 3,
        scratch_shapes=[pltpu.SemaphoreType.DMA((3,)), pltpu.SemaphoreType.DMA((3,))],
        compiler_params=pltpu.CompilerParams(collective_id=1, has_side_effects=True),
        name="swap_windows",
    )(below, above, beyond)


def rows_of(entries):
    full = jnp.concatenate(
        [
            entries,
            entries[0:1] * entries,
            entries[1:2] * entries,
            entries[2:3] * entries,
            jnp.ones_like(entries),
        ],
        axis=0,
    )
    first = full.astype(jnp.bfloat16).astype(jnp.float32)
    rest = full - first
    second = rest.astype(jnp.bfloat16).astype(jnp.float32)
    third = rest - second
    return jnp.concatenate([first, second, third], axis=0).astype(jnp.bfloat16)


def moment_rows(sums, entries, scale):
    sums = sums[0:40] + sums[40:80] + sums[80:120]
    plain, total = sums[0:8], sums[32:33]
    parts = []
    for k in range(3):
        own = entries[k : k + 1]
        parts.append(
            sums[8 * k + 8 : 8 * k + 16]
            - own * plain
            - entries * sums[k : k + 1]
            + own * (entries * total)
        )
    parts.append(sums[32:40])
    return scale * jnp.concatenate(parts, axis=0)


def displaced(entries, row, gap_x, gap_y, gap_v):
    entries = jnp.where(entries > DEAD_ABOVE, -entries, entries)
    return entries + jnp.where(
        row == 0, gap_x, jnp.where(row == 1, gap_y, jnp.where(row == 4, gap_v, 0.0))
    )


def weights(dx, dy, dz):
    dist_sq = jnp.maximum(dx * dx + dy * dy + dz * dz, TINY)
    scaled = dist_sq * lax.rsqrt(dist_sq) * (1.0 / SUPPORT)
    inside = jnp.maximum(1.0 - scaled, 0.0)
    inside = inside * inside
    return inside * inside * (1.0 + 4.0 * scaled)


def finish(sums, entries):
    live = (entries[0:1] < DEAD_ABOVE).astype(jnp.float32)
    number = sums[24:25] + 1.0 - live
    inverse = 1.0 / number
    xx = sums[0:1] * inverse + MOMENT_REG
    xy = sums[1:2] * inverse
    xz = sums[2:3] * inverse
    yy = sums[9:10] * inverse + MOMENT_REG
    yz = sums[10:11] * inverse
    zz = sums[18:19] * inverse + MOMENT_REG
    minor_xx = yy * zz - yz * yz
    minor_xy = xz * yz - xy * zz
    minor_xz = xy * yz - xz * yy
    minor_yy = xx * zz - xz * xz
    minor_yz = xy * xz - xx * yz
    minor_zz = xx * yy - xy * xy
    unit = 1.0 / (xx * minor_xx + xy * minor_xy + xz * minor_xz)
    ixx, ixy, ixz = minor_xx * unit, minor_xy * unit, minor_xz * unit
    iyy, iyz, izz = minor_yy * unit, minor_yz * unit, minor_zz * unit
    half = 0.5 * inverse
    mx, my, mz = sums[0:8] * half, sums[8:16] * half, sums[16:24] * half
    slope_x = ixx * mx + ixy * my + ixz * mz
    slope_y = ixy * mx + iyy * my + iyz * mz
    slope_z = ixz * mx + iyz * my + izz * mz
    scale = KERNEL_NORM * inverse * inverse
    return jnp.concatenate(
        [
            entries,
            slope_x,
            slope_y,
            slope_z,
            ixx * scale,
            ixy * scale,
            ixz * scale,
            iyy * scale,
            iyz * scale,
            izz * scale,
            number,
            number,
        ],
        axis=0,
    )


FLUX_ROWS = (
    tuple(range(8))
    + tuple(8 * k + 11 + q for q in range(5) for k in range(3))
    + tuple(range(32, 38))
)


def flux_terms(near, far, weight):
    d = [far(k) - near(k) for k in range(3)]
    smooth = weights(d[0], d[1], d[2])
    mxx, mxy, mxz, myy, myz, mzz = [near(23 + k) + far(23 + k) for k in range(6)]
    area = [
        smooth * (mxx * d[0] + mxy * d[1] + mxz * d[2]),
        smooth * (mxy * d[0] + myy * d[1] + myz * d[2]),
        smooth * (mxz * d[0] + myz * d[1] + mzz * d[2]),
    ]
    area_sq = area[0] * area[0] + area[1] * area[1] + area[2] * area[2]
    root = lax.rsqrt(jnp.maximum(area_sq, TINY))
    size = area_sq * root * weight
    root = jnp.minimum(root, 1.0 / AREA_FLOOR)
    normal = [area[k] * root for k in range(3)]

    def slope(side, q):
        return side(8 + 3 * q) * d[0] + side(9 + 3 * q) * d[1] + side(10 + 3 * q) * d[2]

    left_vel, right_vel, face = [], [], []
    for q in range(3):
        a, b = near(3 + q), far(3 + q)
        face.append(a + b)
        gap = b - a
        high = jnp.abs(gap)
        low = -high
        left_vel.append(jnp.minimum(jnp.maximum(slope(near, q) - gap, low), high))
        right_vel.append(jnp.minimum(jnp.maximum(gap - slope(far, q), low), high))
    states = []
    for q in (3, 4):
        a, b = near(3 + q), far(3 + q)
        low, high = jnp.minimum(a, b), jnp.maximum(a, b)
        states.append(jnp.minimum(jnp.maximum(a + slope(near, q), low), high))
        states.append(jnp.minimum(jnp.maximum(b - slope(far, q), low), high))
    left_rho, right_rho, left_p, right_p = states
    left_un = left_vel[0] * normal[0] + left_vel[1] * normal[1] + left_vel[2] * normal[2]
    right_un = right_vel[0] * normal[0] + right_vel[1] * normal[1] + right_vel[2] * normal[2]
    root_gamma = math.sqrt(GAMMA)
    left_c = root_gamma * left_p * lax.rsqrt(left_p * left_rho)
    right_c = root_gamma * right_p * lax.rsqrt(right_p * right_rho)
    speed_left = jnp.minimum(left_un - left_c, right_un - right_c)
    speed_right = jnp.maximum(left_un + left_c, right_un + right_c)
    left_m = left_rho * (speed_left - left_un)
    right_m = right_rho * (speed_right - right_un)
    top = right_p - left_p + left_m * left_un - right_m * right_un
    bottom = left_m - right_m
    is_left = top <= 0.0

    def pick(left, right):
        return jnp.where(is_left, left, right)

    rho, p, un = pick(left_rho, right_rho), pick(left_p, right_p), pick(left_un, right_un)
    m, c, speed = pick(left_m, right_m), pick(left_c, right_c), pick(speed_left, speed_right)
    wave = pick(jnp.minimum(speed_left, 0.0), jnp.maximum(speed_right, 0.0))
    lab = [pick(left_vel[k], right_vel[k]) + face[k] for k in range(3)]
    lead = speed * bottom - top
    joint = 1.0 / (bottom * lead)
    contact = top * (lead * joint)
    spread = bottom * (bottom * joint)
    push = wave * ((contact - un) * spread)
    mass = (rho * un + wave * (m * spread - rho)) * size
    thrust = (p + push * m) * size
    carried = (1.5 / GAMMA) * (c * c) + 0.5 * (
        lab[0] * lab[0] + lab[1] * lab[1] + lab[2] * lab[2]
    )
    drift = face[0] * normal[0] + face[1] * normal[1] + face[2] * normal[2]
    energy = mass * carried + drift * thrust + size * (p * un + push * (m * contact + p))
    return [mass] + [lab[k] * mass + normal[k] * thrust for k in range(3)] + [energy]


def pair_kernel(
    slabs,
    subs,
    meta,
    counts,
    number_tab,
    offset_tab,
    below,
    own,
    above,
    beyond,
    own_out,
    above_out,
    store,
    moments,
    near_xyz,
    finished,
    near_rows,
    far_rows,
    row_sums,
    flux_sums,
):
    slab, sub, shear = meta[0], meta[1], meta[2]
    slab_leaves = counts.shape[0]
    homes = slab_leaves // subs
    row = lax.broadcasted_iota(jnp.int32, (8, LEAF), 0)
    for level, source in enumerate((below, own, above, beyond)):
        store[pl.ds(level * WIN, WIN)] = source[...]
    moments[...] = jnp.zeros_like(moments)
    flux_sums[...] = jnp.zeros_like(flux_sums)

    def home_facts(leaf):
        level = leaf // WIN
        place = leaf - level * WIN - 2
        level_slab = lax.rem(slab - 1 + level + slabs, slabs)
        shift = jnp.where(
            (level == 0) & (slab == 0),
            -shear,
            jnp.where((level == 2) & (slab == slabs - 1), shear, 0),
        )
        column = lax.rem(sub * homes + place + shift + 2 * slab_leaves, slab_leaves)
        return level, place, column, level_slab == slabs - 1

    def pair_facts(leaf, kind, facts):
        level, place, column, last = facts
        entry = (level * slab_leaves + column) * KINDS + kind
        crossing = kind >= 2
        step = jnp.where(crossing, kind - 3, jnp.where(kind == 1, 1, 0))
        wraps = crossing & last
        other_column = lax.rem(
            column + step + jnp.where(wraps, shear, 0) + slab_leaves, slab_leaves
        )
        other = leaf + step + jnp.where(crossing, WIN, 0)
        gap_x = jnp.where(crossing, 1.0, 0.0).astype(jnp.float32)
        gap_y = (other_column + offset_tab[entry] - column).astype(jnp.float32)
        gap_v = jnp.where(wraps, -1.0, 0.0).astype(jnp.float32)
        scale = number_tab[entry].astype(jnp.float32) * jnp.where(kind == 0, 0.5, 1.0).astype(
            jnp.float32
        )
        return number_tab[entry], other, place + step, crossing, gap_x, gap_y, gap_v, scale

    def wanted(level, place):
        return ((level == 1) & (place >= 0) & (place <= homes)) | (
            (level == 2) & (place >= -1) & (place <= homes)
        )

    def moment_home(leaf, carry):
        facts = home_facts(leaf)
        level, place = facts[0], facts[1]
        mine = store[leaf]
        turned = jnp.transpose(mine)
        for k in range(3):
            near_xyz[k] = jnp.broadcast_to(turned[:, k : k + 1], (LEAF, LEAF))

        def one(kind, carry):
            number, other, other_place, crossing, gap_x, gap_y, gap_v, scale = pair_facts(
                leaf, kind, facts
            )
            other_level = level + jnp.where(crossing, 1, 0)
            use = (number > 0) & (wanted(level, place) | wanted(other_level, other_place))

            @pl.when(use)
            def _():
                theirs = displaced(store[other], row, gap_x, gap_y, gap_v)
                smooth = weights(
                    theirs[0:1] - near_xyz[0],
                    theirs[1:2] - near_xyz[1],
                    theirs[2:3] - near_xyz[2],
                )
                high = smooth.astype(jnp.bfloat16)
                low = (smooth - high.astype(jnp.float32)).astype(jnp.bfloat16)
                near_part, far_part = rows_of(mine), rows_of(theirs)
                across = (((1,), (1,)), ((), ()))
                along = (((1,), (0,)), ((), ()))

                def times(part, matrix, dims):
                    return lax.dot_general(
                        part, matrix, dims, preferred_element_type=jnp.float32
                    )

                to_near = times(far_part, high, across) + times(far_part, low, across)
                to_far = times(near_part, high, along) + times(near_part, low, along)
                scaled = scale * KERNEL_NORM
                moments[leaf] = moments[leaf] + moment_rows(to_near, mine, scaled)
                moments[other] = moments[other] + moment_rows(to_far, theirs, scaled)

            return carry

        return lax.fori_loop(0, KINDS, one, carry)

    lax.fori_loop(0, 3 * WIN, moment_home, 0)

    own_first, above_first = WIN + 2, 2 * WIN + 1
    halves = jnp.where((row >= 3) & (row < 6), 0.5, 1.0).astype(jnp.float32)

    def finish_one(k, carry):
        leaf = jnp.where(k <= homes, own_first + k, above_first + k - (homes + 1))
        mine = store[leaf]
        done = finish(moments[leaf], mine)
        finished[leaf] = done
        finished[leaf, 0:8] = mine * halves
        return carry

    lax.fori_loop(0, 2 * homes + 3, finish_one, 0)
    ones = jnp.ones((8, LEAF), jnp.float32)

    def flux_home(place, carry):
        leaf = own_first + place
        facts = home_facts(leaf)
        turned = jnp.transpose(finished[leaf])
        for k, source in enumerate(FLUX_ROWS):
            near_rows[k] = jnp.broadcast_to(turned[:, source : source + 1], (LEAF, LEAF)).reshape(
                LEAF // 8, 8, LEAF
            )
        row_sums[...] = jnp.zeros_like(row_sums)
        steps = (counts[facts[2]] + 8 * BLOCK - 1) // (8 * BLOCK)

        def one(kind, carry):
            number, other, _, _, gap_x, gap_y, gap_v, scale = pair_facts(leaf, kind, facts)

            @pl.when(number > 0)
            def _():
                theirs = finished[other]
                head = displaced(theirs[0:8], row, gap_x, gap_y, 0.5 * gap_v)
                for k, source in enumerate(FLUX_ROWS):
                    part = head if source < 8 else theirs
                    far_rows[k] = jnp.broadcast_to(part[source : source + 1], (8, LEAF))

                def step(group, sums):
                    first = group * BLOCK

                    def near(k):
                        return near_rows[k, pl.ds(first, BLOCK)]

                    def far(k):
                        return far_rows[k][None]

                    terms = flux_terms(near, far, scale)
                    totals = []
                    for k in range(5):
                        row_sums[k, pl.ds(first, BLOCK)] += terms[k]
                        totals.append(sums[k] + jnp.sum(terms[k], axis=0))
                    return tuple(totals)

                empty = jnp.zeros((8, LEAF), jnp.float32)
                sums = lax.fori_loop(0, steps, step, (empty,) * 5)
                added = [jnp.sum(part, axis=0, keepdims=True) for part in sums]
                nothing = jnp.zeros((3, LEAF), jnp.float32)
                flux_sums[other] = flux_sums[other] + jnp.concatenate(added + [nothing], axis=0)

            return carry

        lax.fori_loop(0, KINDS, one, 0)
        taken = []
        for k in range(5):
            total = lax.dot_general(
                ones,
                row_sums[k].reshape(LEAF, LEAF),
                (((1,), (1,)), ((), ())),
                precision=HIGHEST,
                preferred_element_type=jnp.float32,
            )
            taken.append(total[0:1])
        nothing = jnp.zeros((3, LEAF), jnp.float32)
        flux_sums[leaf] = flux_sums[leaf] - jnp.concatenate(taken + [nothing], axis=0)
        return carry

    lax.fori_loop(0, homes, flux_home, 0)
    for k in range(homes + 1):
        own_out[k] = flux_sums[own_first + k]
        own_out[k, 5:6, :] = finished[own_first + k, 38:39, :]
    for k in range(homes + 2):
        above_out[k] = flux_sums[above_first + k]


def pair_sums(meta, counts, number_tab, offset_tab, windows, slabs, subs):
    homes = counts.shape[0] // subs
    leaves = LEVELS * WIN
    return pl.pallas_call(
        functools.partial(pair_kernel, slabs, subs),
        out_shape=(
            jax.ShapeDtypeStruct((homes + 1, 8, LEAF), jnp.float32),
            jax.ShapeDtypeStruct((homes + 2, 8, LEAF), jnp.float32),
        ),
        in_specs=[SMEM] * 4 + [VMEM] * 4,
        out_specs=(VMEM, VMEM),
        scratch_shapes=[
            pltpu.VMEM((leaves, 8, LEAF), jnp.float32),
            pltpu.VMEM((leaves, 32, LEAF), jnp.float32),
            pltpu.VMEM((3, LEAF, LEAF), jnp.float32),
            pltpu.VMEM((leaves, 40, LEAF), jnp.float32),
            pltpu.VMEM((len(FLUX_ROWS), LEAF // 8, 8, LEAF), jnp.float32),
            pltpu.VMEM((len(FLUX_ROWS), 8, LEAF), jnp.float32),
            pltpu.VMEM((5, LEAF // 8, 8, LEAF), jnp.float32),
            pltpu.VMEM((leaves, 8, LEAF), jnp.float32),
        ],
        name="pair_sums",
    )(meta, counts, number_tab, offset_tab, *windows)


def collect_kernel(
    slabs, subs, own, above, all_own, all_below, up_sem, ring_send, ring_recv, core_send, core_recv
):
    slab = lax.axis_index("slab")
    sub = lax.axis_index("sub")
    chips = subs // 2
    chip, core = sub // 2, lax.rem(sub, 2)
    partner = 1 - core
    ahead, behind = around(chip + 1, chips), around(chip - 1, chips)
    right_hops = chips // 2
    left_hops = chips - 1 - right_hops
    barrier = pltpu.get_barrier_semaphore()
    for peer in (
        (around(slab + 1, slabs), sub),
        (around(slab - 1, slabs), sub),
        (slab, 2 * ahead + core),
        (slab, 2 * behind + core),
        (slab, 2 * chip + partner),
    ):
        pl.semaphore_signal(barrier, inc=1, device_id=peer, device_id_type=MESH)
    pl.semaphore_wait(barrier, 5)

    upward = pltpu.make_async_remote_copy(
        src_ref=above,
        dst_ref=all_below.at[sub],
        send_sem=up_sem.at[0],
        recv_sem=up_sem.at[1],
        device_id=(around(slab + 1, slabs), sub),
        device_id_type=MESH,
    )
    upward.start()
    mine = pltpu.make_async_copy(own, all_own.at[sub], up_sem.at[2])
    mine.start()

    def ring(which, source, buffer, owner_chip, hop, to_right):
        slot = 2 * owner_chip + core
        place = (hop - 1) if to_right else (right_hops + hop - 1)
        return pltpu.make_async_remote_copy(
            src_ref=source if source is not None else buffer.at[slot],
            dst_ref=buffer.at[slot],
            send_sem=ring_send.at[which, place],
            recv_sem=ring_recv.at[which, place],
            device_id=(slab, 2 * (ahead if to_right else behind) + core),
            device_id_type=MESH,
        )

    def across(which, source, buffer, owner_chip, place):
        slot = 2 * owner_chip + core
        return pltpu.make_async_remote_copy(
            src_ref=source if source is not None else buffer.at[slot],
            dst_ref=buffer.at[slot],
            send_sem=core_send.at[which, place],
            recv_sem=core_recv.at[which, place],
            device_id=(slab, 2 * chip + partner),
            device_id_type=MESH,
        )

    started, expected = [], []

    def launch(which, source, buffer):
        for to_right, hops in ((True, right_hops), (False, left_hops)):
            if hops > 0:
                one = ring(which, source, buffer, chip, 1, to_right)
                one.start()
                started.append(one)
        one = across(which, source, buffer, chip, 0)
        one.start()
        started.append(one)
        expected.append(one)

    launch(0, own, all_own)
    upward.wait()
    launch(1, None, all_below)
    mine.wait()
    for hop in range(1, right_hops + 1):
        for which, buffer in ((0, all_own), (1, all_below)):
            for to_right, hops in ((True, right_hops), (False, left_hops)):
                if hop > hops:
                    continue
                owner = around(chip - hop, chips) if to_right else around(chip + hop, chips)
                ring(which, None, buffer, owner, hop, to_right).wait_recv()
                if hop < hops:
                    one = ring(which, None, buffer, owner, hop + 1, to_right)
                    one.start()
                    started.append(one)
                place = hop if to_right else right_hops + hop
                one = across(which, None, buffer, owner, place)
                one.start()
                started.append(one)
                expected.append(one)
    for one in expected:
        one.wait_recv()
    for one in started:
        one.wait_send()


def collect_sums(own, above, slabs, subs):
    chips = subs // 2
    return pl.pallas_call(
        functools.partial(collect_kernel, slabs, subs),
        out_shape=(
            jax.ShapeDtypeStruct((subs,) + own.shape, jnp.float32),
            jax.ShapeDtypeStruct((subs,) + above.shape, jnp.float32),
        ),
        in_specs=[VMEM, VMEM],
        out_specs=(VMEM, VMEM),
        scratch_shapes=[
            pltpu.SemaphoreType.DMA((3,)),
            pltpu.SemaphoreType.DMA((2, chips)),
            pltpu.SemaphoreType.DMA((2, chips)),
            pltpu.SemaphoreType.DMA((2, chips)),
            pltpu.SemaphoreType.DMA((2, chips)),
        ],
        compiler_params=pltpu.CompilerParams(collective_id=2, has_side_effects=True),
        name="collect_sums",
    )(own, above)


def total_kernel(subs, meta, all_own, all_below, out):
    slab, shear = meta[0], jnp.where(meta[0] == 0, meta[2], 0)
    homes = all_own.shape[1] - 1
    slab_leaves = subs * homes

    def one(column, carry):
        device, place = column // homes, lax.rem(column, homes)
        mine = all_own[device, place]
        before = all_own[lax.rem(device + subs - 1, subs), homes]
        total = mine + jnp.where(place == 0, 1.0, 0.0).astype(jnp.float32) * before
        source = lax.rem(column - shear + slab_leaves, slab_leaves)
        device, place = source // homes, lax.rem(source, homes)
        total = total + all_below[device, place + 1]
        nearer = all_below[lax.rem(device + subs - 1, subs), homes + 1]
        later = all_below[lax.rem(device + 1, subs), 0]
        total = total + jnp.where(place == 0, 1.0, 0.0).astype(jnp.float32) * nearer
        total = total + jnp.where(place == homes - 1, 1.0, 0.0).astype(jnp.float32) * later
        start = pl.multiple_of(column * LEAF, LEAF)
        out[:, pl.ds(start, LEAF)] = total[0:5] * mine[5:6]
        return carry

    lax.fori_loop(0, slab_leaves, one, 0)


def total_rates(meta, all_own, all_below, subs):
    homes = all_own.shape[1] - 1
    return pl.pallas_call(
        functools.partial(total_kernel, subs),
        out_shape=jax.ShapeDtypeStruct((5, subs * homes * LEAF), jnp.float32),
        in_specs=[SMEM, VMEM, VMEM],
        out_specs=VMEM,
        name="total_rates",
    )(meta, all_own, all_below)


def shards(slabs, subs, positions, velocity, density, pressure, counts, pair_list):
    slab_leaves = counts.shape[0]
    slots = pair_list.shape[1]
    slab, sub = lax.axis_index("slab"), lax.axis_index("sub")
    row = jnp.pad(pair_list.reshape(-1), (0, LEAF - 3 * slots)).reshape(1, 1, LEAF)
    lists = gather_lists(row, slabs, subs)
    shear, number_tab, offset_tab = pair_tables(lists, slab, slabs, slots, slab_leaves)
    meta = jnp.stack([slab, sub, shear, shear]).astype(jnp.int32)
    own, to_up, to_down, to_second = leaf_windows(
        meta,
        counts,
        positions,
        velocity,
        density.reshape(slab_leaves, LEAF),
        pressure.reshape(slab_leaves, LEAF),
        slabs,
        subs,
    )
    below, above, beyond = swap_windows(to_up, to_down, to_second, slabs)
    own_part, above_part = pair_sums(
        meta, counts, number_tab, offset_tab, (below, own, above, beyond), slabs, subs
    )
    all_own, all_below = collect_sums(own_part, above_part, slabs, subs)
    return total_rates(meta, all_own, all_below, subs)


def solution(mesh):
    placed = (
        P(None, "slab"),
        P(None, "slab"),
        P("slab"),
        P("slab"),
        P("slab"),
        P(None, ("slab", "sub")),
    )
    return jax.shard_map(
        functools.partial(shards, mesh.shape["slab"], mesh.shape["sub"]),
        mesh=mesh,
        in_specs=placed,
        out_specs=P(None, "slab"),
        check_vma=False,
    )
```

time: 1030 us -> 158 us (0.15)
  local copies, waits for them, and re-layouts: 334 us -> 2.72 us
  waiting for transfers between devices: 322 us -> 0 us
  other arithmetic: 318 us -> 4.63 us
  Pallas kernels: 0 us -> 153 us
  starting transfers between devices: 20.2 us -> 0 us
  between operations: 14.4 us -> 0.05 us
  loops' own time: 12.5 us -> 0 us
    reduce_sum x57 -> x0, other arithmetic: 277 us -> none  [the longest x40 246 us: flux_tile(): jnp.sum(pair_scale * face_flux, axis=1)]
    psum x2 -> x0, waiting for transfers between devices: 244 us -> none  [settle(): partial_value = lax.psum(partial_value, 'sub')]
    while x1648 -> x0, local copies, waits for them, and re-layouts: 234 us -> none
    pallas_call x0 -> x6, Pallas kernels: none -> 153 us  [the longest x1 73.5 us: pair_sums(): pl.pallas_call(functools.partial(pair_kernel, slabs, subs), out_shape=(ja...]
    ppermute x5 -> x0, waiting for transfers between devices: 77.5 us -> none  [shifted(): lax.ppermute(shard, axis, [(i, (i + by) % peers) for i in range(peers)])]
    gather x81 -> x0, local copies, waits for them, and re-layouts: 64.3 us -> none  [the longest x8 14.2 us: flux_fn(): jnp.take(window, other_part, axis=1)]
    ppermute x5 -> x0, starting transfers between devices: 20.2 us -> none  [shifted(): lax.ppermute(shard, axis, [(i, (i + by) % peers) for i in range(peers)])]
    dynamic_update_slice x32 -> x0, local copies, waits for them, and re-layouts: 15.3 us -> none  [the longest x16 12.7 us: one_turn(): lax.dynamic_update_slice_in_dim(row_buffer, row_sums, first_slot, 1)]
  transfers between devices with their start and end apart: 7 -> 0, of which waited for: 6 -> 0; matrix products, arithmetic and copies ran while one was open for 1% -> 0% of each run, Pallas kernels for 0% -> 0%
where the time goes in v1:
time: 158 us; the launch traced here: 160 us
  Pallas kernels  153 us (97%)
  other arithmetic  4.63 us (3%)
  local copies, waits for them, and re-layouts  2.72 us (2%)
    pallas_call x1, Pallas kernels, pair_sums(): pl.pallas_call(functools.partial(pair_kernel, slabs, subs), out_shape=(ja...  73.5 us
    pallas_call x1, Pallas kernels, collect_sums(): pl.pallas_call(functools.partial(collect_kernel, slabs, subs), out_shape=...  36.8 us
    pallas_call x1, Pallas kernels, gather_lists(): pl.pallas_call(functools.partial(gather_kernel, slabs, subs), out_shape=j...  25.2 us
    pallas_call x1, Pallas kernels, swap_windows(): pl.pallas_call(functools.partial(swap_kernel, slabs), out_shape=(window,)...  9.07 us
    pallas_call x1, Pallas kernels, total_rates(): pl.pallas_call(functools.partial(total_kernel, subs), out_shape=jax.Shape...  5.78 us

profile of v1, /device:TPU:1, one launch (start us, length us, event | category | flops | bytes accessed | tf_op | source)
XLA Modules:
  0.0 160.0 jit_solution(9996269385839463524)
XLA Ops:
  0.0 0.0 copy-start.1
  0.0 0.7 copy-done.1
  0.7 0.1 reshape.23
  0.8 0.5 pad_bitcast_fusion.row_ref
  1.3 25.2 %gather_lists.1 = s32[64,1,128]{2,1,0:T(1,128)} custom-call(s32[1,1,128]{2,1,0:T(1,128)} %pad_bitcast_fusion.row_ref), custom_call_target="tpu_custom_call" | custom-call | tf_op jit(solution)/shard_map/gather_lists/pallas_call | solution.py:102
  26.5 0.0 copy-start
  26.5 0.8 broadcast_compare_fusion
  27.3 0.0 copy-done
  27.3 0.1 slice.30
  27.4 0.8 negate_select_fusion.2
  28.2 1.3 pad_add_fusion.meta
  29.5 1.7 %select_reduce_fusion = (s32[3,16,40]{2,1,0:T(8,128)S(1)}, s32[3,16,40]{2,1,0:T(8,128)S(1)}) fusion(s32[3,16,40]{2,1,0:T(8,128)S(1)} %slice.30, s32[3,16,40]{2,1,0:T(8,128)S(1)} %fusion.14), kind=kLoop, calls=%fused_computation | loop fusion | flops 380160 | bytes 30720 | tf_op jit(solution)/shard_map/reduce_max | solution.py:137
  31.2 0.7 reshape.27.offset_tab
  31.9 0.7 reshape.26.number_tab
  32.6 2.2 %leaf_windows.1 = (f32[12,8,128]{2,1,0:T(8,128)}, f32[12,8,128]{2,1,0:T(8,128)}, f32[12,8,128]{2,1,0:T(8,128)}, f32[12,8,128]{2,1,0:T(8,128)}) custom-call(s32[4]{0:T(128)} %pad_add_fusion.meta, s32[128]{0:T(128)} %counts.3, f32[3,16384]{1,0:T(4,128)} %positions.1, f32[3,16384]{1,0:T(4,128)} %velocity.1, f32[128,128]{1,0:T(8,128)} %bitcast.11, ...), custom_call_target="tpu_custom_call" | custom-call | tf_op jit(solution)/shard_map/leaf_windows/pallas_call | solution.py:180
  34.8 9.1 %swap_windows.1 = (f32[12,8,128]{2,1,0:T(8,128)}, f32[12,8,128]{2,1,0:T(8,128)}, f32[12,8,128]{2,1,0:T(8,128)}) custom-call(f32[12,8,128]{2,1,0:T(8,128)} %get-tuple-element.16.below, f32[12,8,128]{2,1,0:T(8,128)} %get-tuple-element.17.above, f32[12,8,128]{2,1,0:T(8,128)} %get-tuple-element.18.beyond), custom_call_target="tpu_custom_call" | custom-call | tf_op jit(solution)/shard_map/swap_windows/pallas_call | solution.py:221
  43.9 73.5 %pair_sums.1 = (f32[9,8,128]{2,1,0:T(8,128)}, f32[10,8,128]{2,1,0:T(8,128)}) custom-call(s32[4]{0:T(128)} %pad_add_fusion.meta, s32[128]{0:T(128)} %counts.3, s32[1920]{0:T(1024)} %reshape.26.number_tab, s32[1920]{0:T(1024)} %reshape.27.offset_tab, f32[12,8,128]{2,1,0:T(8,128)} %get-tuple-element.19.below, f32[12,8,128]{2,1,0:T(8,128)} %get-tuple-element.20.own, ...), custom_call_target="tpu_custom_call" | custom-call | tf_op jit(solution)/shard_map/pair_sums/pallas_call | solution.py:599
  117.5 36.8 %collect_sums.1 = (f32[16,9,8,128]{3,2,1,0:T(8,128)}, f32[16,10,8,128]{3,2,1,0:T(8,128)}) custom-call(f32[9,8,128]{2,1,0:T(8,128)} %get-tuple-element.23.own, f32[10,8,128]{2,1,0:T(8,128)} %get-tuple-element.24.above), custom_call_target="tpu_custom_call" | custom-call | tf_op jit(solution)/shard_map/collect_sums/pallas_call | solution.py:719
  154.2 5.8 %total_rates.1 = f32[5,16384]{1,0:T(8,128)} custom-call(s32[4]{0:T(128)} %pad_add_fusion.meta, f32[16,9,8,128]{3,2,1,0:T(8,128)} %get-tuple-element.25.all_own, f32[16,10,8,128]{3,2,1,0:T(8,128)} %get-tuple-element.26.all_below), custom_call_target="tpu_custom_call" | custom-call | tf_op jit(solution)/shard_map/total_rates/pallas_call | solution.py:765
  (1 shorter events, 0.0 us)
Async XLA Ops:
  0.0 0.7 copy-start.1
  26.5 0.8 copy-start

commit v2 on v1

v2 whole, which is shorter than its diff:
```python
import functools
import math

import jax
import jax.numpy as jnp
from jax import lax
from jax.experimental import pallas as pl
from jax.experimental.pallas import tpu as pltpu
from jax.sharding import PartitionSpec as P

LEAF = 128
KINDS = 5
WIN = 12
LEVELS = 4
GAMMA = 5.0 / 3.0
SUPPORT = 1.5
KERNEL_NORM = 21.0 / (2.0 * math.pi * SUPPORT**3)
MOMENT_REG = 0.05
AREA_FLOOR = 0.0001
FAR_AWAY = 1.0e6
DEAD_ABOVE = 1.0e5
TINY = 1.2e-38
BLOCK = 2
MESH = pl.DeviceIdType.MESH
VMEM = pl.BlockSpec(memory_space=pltpu.VMEM)
SMEM = pl.BlockSpec(memory_space=pltpu.SMEM)
HIGHEST = lax.Precision.HIGHEST


def around(value, size):
    return lax.rem(value + size, size)


def table_row(pair_list, slab, slabs, slab_leaves, homes):
    home, other, offset = pair_list[0], pair_list[1], pair_list[2]
    occupied = home >= 0
    crossing = occupied & (home // slab_leaves != other // slab_leaves)
    step = (other - home + offset + 1) & (slab_leaves - 1)
    kind = jnp.where(other == home, 0, jnp.where(crossing, 2 + step, 1))
    key = jnp.where(occupied & (kind < KINDS), (home & (homes - 1)) * KINDS + kind, -1)
    shear = jnp.where(crossing & (slab == slabs - 1), (-offset) & (slab_leaves - 1), 0)
    lane = jnp.arange(LEAF, dtype=jnp.int32)[:, None]
    size = homes * KINDS
    number = jnp.where(key[None] == lane, 1, 0)
    moved = jnp.where(key[None] == lane - size, offset[None], 0)
    shears = jnp.where(lane == 2 * size, shear[None], 0)
    signed = jnp.where((lane >= size) & (lane < 2 * size) & (moved < 0), moved, 0)
    row = jnp.sum(number, axis=1) + jnp.max(moved + shears, axis=1) + jnp.min(signed, axis=1)
    return row.reshape(1, 1, LEAF)


def exchange_kernel(
    slabs,
    subs,
    row_ref,
    counts,
    positions,
    velocity,
    density,
    pressure,
    lists,
    own,
    below,
    above,
    beyond,
    to_up,
    to_down,
    to_second,
    records,
    list_sems,
    window_sems,
):
    slab = lax.axis_index("slab")
    sub = lax.axis_index("sub")
    slab_leaves = counts.shape[0]
    homes = slab_leaves // subs
    barrier = pltpu.get_barrier_semaphore()

    def each_sub(first, body):
        def one(k, carry):
            body(k)
            return carry

        lax.fori_loop(first, subs, one, 0, unroll=4 if first == 0 else 5)

    for shift in (-2, -1, 0, 1, 2):
        peer_slab = (slab + shift + slabs) & (slabs - 1)

        def greet(k, peer_slab=peer_slab):
            pl.semaphore_signal(
                barrier,
                inc=1,
                device_id=(peer_slab, (sub + k) & (subs - 1)),
                device_id_type=MESH,
            )

        each_sub(1 if shift == 0 else 0, greet)

    lane = lax.broadcasted_iota(jnp.int32, (1, LEAF), 1)
    row = lax.broadcasted_iota(jnp.int32, (3, LEAF), 0)

    def record(leaf, carry):
        start = pl.multiple_of(leaf * LEAF, LEAF)
        live = lane < counts[leaf]
        centre = jnp.where(
            row == 0,
            slab.astype(jnp.float32) + 0.5,
            jnp.where(row == 1, leaf.astype(jnp.float32) + 0.5, 0.5),
        )
        place = (positions[:, pl.ds(start, LEAF)] - centre) * (1.0 / SUPPORT)
        records[leaf, 0:3, :] = jnp.where((row > 0) | live, place, FAR_AWAY)
        records[leaf, 3:6, :] = velocity[:, pl.ds(start, LEAF)]
        records[leaf, 6:7, :] = density[pl.ds(leaf, 1), :]
        records[leaf, 7:8, :] = pressure[pl.ds(leaf, 1), :]
        return carry

    lax.fori_loop(0, slab_leaves, record, 0, unroll=4)

    def fill(target, shift):
        first = sub * homes - 2 + shift + 2 * slab_leaves
        for slot in range(WIN):
            target[slot] = records[(first + slot) & (slab_leaves - 1)]

    fill(own, 0)
    pl.semaphore_wait(barrier, 5 * subs - 1)
    mine = pltpu.make_async_copy(
        row_ref, lists.at[pl.ds(2 * subs + sub, 1)], list_sems.at[2]
    )
    mine.start()
    for shift in (-2, 1, -1, 0):
        peer_slab = (slab - shift + slabs) & (slabs - 1)

        def send(k, shift=shift, peer_slab=peer_slab):
            pltpu.make_async_remote_copy(
                src_ref=row_ref,
                dst_ref=lists.at[pl.ds((shift + 2) * subs + sub, 1)],
                send_sem=list_sems.at[0],
                recv_sem=list_sems.at[1],
                device_id=(peer_slab, (sub + k) & (subs - 1)),
                device_id_type=MESH,
            ).start()

        each_sub(1 if shift == 0 else 0, send)
    mine.wait()
    rest = lists.at[pl.ds(0, 4 * subs - 1)]
    everything = pltpu.make_async_remote_copy(
        src_ref=rest,
        dst_ref=rest,
        send_sem=list_sems.at[0],
        recv_sem=list_sems.at[1],
        device_id=((slab + 1) & (slabs - 1), sub),
        device_id_type=MESH,
    )
    everything.wait_recv()
    everything.wait_send()
    shear = jnp.max(
        jnp.where(
            lax.broadcasted_iota(jnp.int32, (4 * subs, 1, LEAF), 2) == 2 * homes * KINDS,
            lists[...],
            0,
        )
    )
    copies = []
    for k, (shift, source, target) in enumerate(
        ((-2, to_second, beyond), (-1, to_down, above), (1, to_up, below))
    ):
        copies.append(
            pltpu.make_async_remote_copy(
                src_ref=source,
                dst_ref=target,
                send_sem=window_sems.at[k],
                recv_sem=window_sems.at[3 + k],
                device_id=((slab + shift + slabs) & (slabs - 1), sub),
                device_id_type=MESH,
            )
        )
    none = jnp.int32(0)
    fill(to_second, jnp.where(slab <= 1, shear, none))
    fill(to_down, jnp.where(slab == 0, shear, none))
    copies[0].start()
    fill(to_up, jnp.where(slab == slabs - 1, -shear, none))
    copies[1].start()
    copies[2].start()
    for one in copies:
        one.wait()


def exchange(row, counts, positions, velocity, density, pressure, slabs, subs):
    window = jax.ShapeDtypeStruct((WIN, 8, LEAF), jnp.float32)
    return pl.pallas_call(
        functools.partial(exchange_kernel, slabs, subs),
        out_shape=(jax.ShapeDtypeStruct((4 * subs, 1, LEAF), jnp.int32),) + (window,) * 4,
        in_specs=[VMEM, SMEM, VMEM, VMEM, VMEM, VMEM],
        out_specs=(VMEM,) * 5,
        scratch_shapes=[pltpu.VMEM((WIN, 8, LEAF), jnp.float32)] * 3
        + [pltpu.VMEM((counts.shape[0], 8, LEAF), jnp.float32)]
        + [pltpu.SemaphoreType.DMA((3,)), pltpu.SemaphoreType.DMA((6,))],
        compiler_params=pltpu.CompilerParams(collective_id=0, has_side_effects=True),
        name="exchange",
    )(row, counts, positions, velocity, density, pressure)


def three_parts(full):
    first = full.astype(jnp.bfloat16).astype(jnp.float32)
    rest = full - first
    second = rest.astype(jnp.bfloat16).astype(jnp.float32)
    return first, second, rest - second


def left_stack(full):
    first, second, third = three_parts(full)
    return jnp.concatenate([first, first, second, second, first, third], axis=0).astype(
        jnp.bfloat16
    )


def right_stack(full):
    first, second, third = three_parts(full)
    return jnp.concatenate([first, second, first, second, third, first], axis=0).astype(
        jnp.bfloat16
    )


def features(entries, scale):
    scaled = scale * entries
    full = jnp.concatenate(
        [
            scaled,
            entries[0:1] * scaled,
            entries[1:2] * scaled,
            entries[2:3] * scaled,
            jnp.full_like(entries, scale),
        ],
        axis=0,
    )
    return jnp.concatenate(three_parts(full), axis=0).astype(jnp.bfloat16)


def moment_rows(sums, entries):
    sums = sums[0:40] + sums[40:80] + sums[80:120]
    plain, total = sums[0:8], sums[32:33]
    parts = []
    for k in range(3):
        own = entries[k : k + 1]
        parts.append(
            sums[8 * k + 8 : 8 * k + 16]
            - own * plain
            - entries * sums[k : k + 1]
            + own * (entries * total)
        )
    parts.append(sums[32:40])
    return KERNEL_NORM * jnp.concatenate(parts, axis=0)


def displaced(entries, row, gap_x, gap_y, gap_v):
    entries = jnp.where(entries > DEAD_ABOVE, -entries, entries)
    return entries + jnp.where(
        row == 0, gap_x, jnp.where(row == 1, gap_y, jnp.where(row == 4, gap_v, 0.0))
    )


def length_sq(entries):
    x, y, z = entries[0:1], entries[1:2], entries[2:3]
    return x * x + y * y + z * z


def weights(dist_sq):
    dist_sq = jnp.maximum(dist_sq, TINY)
    inside = jnp.maximum(1.0 - dist_sq * lax.rsqrt(dist_sq), 0.0)
    square = inside * inside
    return square * square * (5.0 - 4.0 * inside)


def finish(sums, entries):
    live = (entries[0:1] < DEAD_ABOVE).astype(jnp.float32)
    number = sums[24:25] + 1.0 - live
    inverse = 1.0 / number
    area = inverse * SUPPORT**2
    xx = sums[0:1] * area + MOMENT_REG
    xy = sums[1:2] * area
    xz = sums[2:3] * area
    yy = sums[9:10] * area + MOMENT_REG
    yz = sums[10:11] * area
    zz = sums[18:19] * area + MOMENT_REG
    minor_xx = yy * zz - yz * yz
    minor_xy = xz * yz - xy * zz
    minor_xz = xy * yz - xz * yy
    minor_yy = xx * zz - xz * xz
    minor_yz = xy * xz - xx * yz
    minor_zz = xx * yy - xy * xy
    unit = 1.0 / (xx * minor_xx + xy * minor_xy + xz * minor_xz)
    ixx, ixy, ixz = minor_xx * unit, minor_xy * unit, minor_xz * unit
    iyy, iyz, izz = minor_yy * unit, minor_yz * unit, minor_zz * unit
    half = 0.5 * area
    mx, my, mz = sums[0:8] * half, sums[8:16] * half, sums[16:24] * half
    slope_x = ixx * mx + ixy * my + ixz * mz
    slope_y = ixy * mx + iyy * my + iyz * mz
    slope_z = ixz * mx + iyz * my + izz * mz
    scale = (KERNEL_NORM * SUPPORT) * inverse * inverse
    return jnp.concatenate(
        [
            entries,
            slope_x,
            slope_y,
            slope_z,
            ixx * scale,
            ixy * scale,
            ixz * scale,
            iyy * scale,
            iyz * scale,
            izz * scale,
            number,
            number,
        ],
        axis=0,
    )


FLUX_ROWS = (
    tuple(range(8))
    + tuple(8 * k + 11 + q for q in range(5) for k in range(3))
    + tuple(range(32, 38))
)


def flux_terms(near, far, weight):
    d = [far(k) - near(k) for k in range(3)]
    smooth = weights(d[0] * d[0] + d[1] * d[1] + d[2] * d[2])
    mxx, mxy, mxz, myy, myz, mzz = [near(23 + k) + far(23 + k) for k in range(6)]
    area = [
        smooth * (mxx * d[0] + mxy * d[1] + mxz * d[2]),
        smooth * (mxy * d[0] + myy * d[1] + myz * d[2]),
        smooth * (mxz * d[0] + myz * d[1] + mzz * d[2]),
    ]
    area_sq = area[0] * area[0] + area[1] * area[1] + area[2] * area[2]
    root = lax.rsqrt(jnp.maximum(area_sq, TINY))
    size = area_sq * root * weight
    root = jnp.minimum(root, 1.0 / AREA_FLOOR)
    normal = [area[k] * root for k in range(3)]

    def slope(side, q):
        return side(8 + 3 * q) * d[0] + side(9 + 3 * q) * d[1] + side(10 + 3 * q) * d[2]

    left_vel, right_vel, face = [], [], []
    for q in range(3):
        a, b = near(3 + q), far(3 + q)
        face.append(a + b)
        gap = b - a
        high = jnp.abs(gap)
        low = -high
        left_vel.append(jnp.minimum(jnp.maximum(slope(near, q) - gap, low), high))
        right_vel.append(jnp.minimum(jnp.maximum(gap - slope(far, q), low), high))
    states = []
    for q in (3, 4):
        a, b = near(3 + q), far(3 + q)
        low, high = jnp.minimum(a, b), jnp.maximum(a, b)
        states.append(jnp.minimum(jnp.maximum(a + slope(near, q), low), high))
        states.append(jnp.minimum(jnp.maximum(b - slope(far, q), low), high))
    left_rho, right_rho, left_p, right_p = states
    left_un = left_vel[0] * normal[0] + left_vel[1] * normal[1] + left_vel[2] * normal[2]
    right_un = right_vel[0] * normal[0] + right_vel[1] * normal[1] + right_vel[2] * normal[2]
    root_gamma = math.sqrt(GAMMA)
    left_c = root_gamma * left_p * lax.rsqrt(left_p * left_rho)
    right_c = root_gamma * right_p * lax.rsqrt(right_p * right_rho)
    speed_left = jnp.minimum(left_un - left_c, right_un - right_c)
    speed_right = jnp.maximum(left_un + left_c, right_un + right_c)
    left_m = left_rho * (speed_left - left_un)
    right_m = right_rho * (speed_right - right_un)
    top = right_p - left_p + left_m * left_un - right_m * right_un
    bottom = left_m - right_m
    is_left = top <= 0.0

    def pick(left, right):
        return jnp.where(is_left, left, right)

    rho, p, un = pick(left_rho, right_rho), pick(left_p, right_p), pick(left_un, right_un)
    m, c, speed = pick(left_m, right_m), pick(left_c, right_c), pick(speed_left, speed_right)
    wave = pick(jnp.minimum(speed_left, 0.0), jnp.maximum(speed_right, 0.0))
    lab = [pick(left_vel[k], right_vel[k]) + face[k] for k in range(3)]
    lead = speed * bottom - top
    joint = 1.0 / (bottom * lead)
    contact = top * (lead * joint)
    spread = bottom * (bottom * joint)
    push = wave * ((contact - un) * spread)
    mass = (rho * un + wave * (m * spread - rho)) * size
    thrust = (p + push * m) * size
    carried = (1.5 / GAMMA) * (c * c) + 0.5 * (
        lab[0] * lab[0] + lab[1] * lab[1] + lab[2] * lab[2]
    )
    drift = face[0] * normal[0] + face[1] * normal[1] + face[2] * normal[2]
    energy = mass * carried + drift * thrust + size * (p * un + push * (m * contact + p))
    return [mass] + [lab[k] * mass + normal[k] * thrust for k in range(3)] + [energy]


def pair_kernel(
    slabs,
    subs,
    tables,
    counts,
    below,
    own,
    above,
    beyond,
    own_out,
    above_out,
    store,
    finished,
    near_rows,
    far_rows,
    row_sums,
    flux_sums,
):
    slab = lax.axis_index("slab")
    sub = lax.axis_index("sub")
    slab_leaves = counts.shape[0]
    homes = slab_leaves // subs
    table_size = homes * KINDS
    row = lax.broadcasted_iota(jnp.int32, (8, LEAF), 0)
    for level, source in enumerate((below, own, above, beyond)):
        store[pl.ds(level * WIN, WIN)] = source[...]
    flux_sums[...] = jnp.zeros_like(flux_sums)

    def most(k, value):
        return jnp.maximum(value, tables[k, 2 * table_size])

    shear = lax.fori_loop(0, 4 * subs, most, jnp.int32(0))

    def home_facts(level, place):
        shift = jnp.where(
            (level == 0) & (slab == 0),
            -shear,
            jnp.where((level == 2) & (slab == slabs - 1), shear, 0),
        )
        column = (sub * homes + place + shift + 2 * slab_leaves) & (slab_leaves - 1)
        level_slab = (slab - 1 + level + slabs) & (slabs - 1)
        return level, column, level_slab == slabs - 1

    def pair_facts(facts, kind):
        level, column, last = facts
        device = (level + 1) * subs + column // homes
        entry = (column & (homes - 1)) * KINDS + kind
        crossing = kind >= 2
        step = jnp.where(crossing, kind - 3, jnp.where(kind == 1, 1, 0))
        wraps = crossing & last
        other_column = (
            column + step + jnp.where(wraps, shear, 0) + slab_leaves
        ) & (slab_leaves - 1)
        gap_x = jnp.where(crossing, 1.0 / SUPPORT, 0.0).astype(jnp.float32)
        gap_y = (other_column + tables[device, table_size + entry] - column).astype(
            jnp.float32
        ) * (1.0 / SUPPORT)
        gap_v = jnp.where(wraps, -1.0, 0.0).astype(jnp.float32)
        return tables[device, entry], step + jnp.where(crossing, WIN, 0), gap_x, gap_y, gap_v

    own_first, above_first = WIN + 2, 2 * WIN + 1
    halves = jnp.where((row >= 3) & (row < 6), 0.5, 1.0).astype(jnp.float32)

    def finish_one(k, carry):
        level = jnp.where(k <= homes, 1, 2)
        place = jnp.where(k <= homes, k, k - (homes + 2))
        leaf = level * WIN + place + 2
        mine = store[leaf]
        near_sq = length_sq(mine)
        left = jnp.where(
            row < 3, -2.0 * mine, jnp.where(row == 3, 1.0, jnp.where(row == 4, near_sq, 0.0))
        )
        left = jnp.transpose(left_stack(left).astype(jnp.float32)).astype(jnp.bfloat16)
        here = home_facts(level, place)
        pairs = [(here, kind, 1) for kind in range(KINDS)]
        pairs.append((home_facts(level, place - 1), 1, -1))
        pairs += [(home_facts(level - 1, place + 3 - kind), kind, -1) for kind in (2, 3, 4)]
        sums = None
        for facts, kind, sign in pairs:
            number, away, gap_x, gap_y, gap_v = pair_facts(facts, kind)
            theirs = displaced(
                store[leaf + sign * away], row, sign * gap_x, sign * gap_y, sign * gap_v
            )
            right = jnp.where(
                row < 3,
                theirs,
                jnp.where(row == 3, length_sq(theirs), jnp.where(row == 4, 1.0, 0.0)),
            )
            smooth = weights(
                lax.dot_general(
                    left,
                    right_stack(right),
                    (((1,), (0,)), ((), ())),
                    preferred_element_type=jnp.float32,
                )
            )
            high = smooth.astype(jnp.bfloat16)
            low = (smooth - high.astype(jnp.float32)).astype(jnp.bfloat16)
            rows = features(theirs, number.astype(jnp.float32))
            part = lax.dot_general(
                jnp.concatenate([rows, rows], axis=1),
                jnp.concatenate([high, low], axis=1),
                (((1,), (1,)), ((), ())),
                preferred_element_type=jnp.float32,
            )
            sums = part if sums is None else sums + part
        finished[leaf] = finish(moment_rows(sums, mine), mine)
        finished[leaf, 0:8] = mine * halves
        return carry

    lax.fori_loop(0, 2 * homes + 3, finish_one, 0)
    ones = jnp.ones((8, LEAF), jnp.float32)

    def flux_home(place, carry):
        leaf = own_first + place
        facts = home_facts(1, place)
        turned = jnp.transpose(finished[leaf])
        for k, source in enumerate(FLUX_ROWS):
            near_rows[k] = jnp.broadcast_to(turned[:, source : source + 1], (LEAF, LEAF)).reshape(
                LEAF // 8, 8, LEAF
            )
        row_sums[...] = jnp.zeros_like(row_sums)
        steps = (counts[facts[1]] + 8 * BLOCK - 1) // (8 * BLOCK)

        def one(kind, carry):
            number, away, gap_x, gap_y, gap_v = pair_facts(facts, kind)
            other = leaf + away
            scale = number.astype(jnp.float32) * jnp.where(kind == 0, 0.5, 1.0).astype(jnp.float32)

            @pl.when(number > 0)
            def _():
                theirs = finished[other]
                head = displaced(theirs[0:8], row, gap_x, gap_y, 0.5 * gap_v)
                for k, source in enumerate(FLUX_ROWS):
                    part = head if source < 8 else theirs
                    far_rows[k] = jnp.broadcast_to(part[source : source + 1], (8, LEAF))

                def step(group, sums):
                    first = group * BLOCK

                    def near(k):
                        return near_rows[k, pl.ds(first, BLOCK)]

                    def far(k):
                        return far_rows[k][None]

                    terms = flux_terms(near, far, scale)
                    totals = []
                    for k in range(5):
                        row_sums[k, pl.ds(first, BLOCK)] += terms[k]
                        totals.append(sums[k] + jnp.sum(terms[k], axis=0))
                    return tuple(totals)

                empty = jnp.zeros((8, LEAF), jnp.float32)
                sums = lax.fori_loop(0, steps, step, (empty,) * 5)
                added = [jnp.sum(part, axis=0, keepdims=True) for part in sums]
                nothing = jnp.zeros((3, LEAF), jnp.float32)
                flux_sums[other] = flux_sums[other] + jnp.concatenate(added + [nothing], axis=0)

            return carry

        lax.fori_loop(0, KINDS, one, 0)
        taken = []
        for k in range(5):
            total = lax.dot_general(
                ones,
                row_sums[k].reshape(LEAF, LEAF),
                (((1,), (1,)), ((), ())),
                precision=HIGHEST,
                preferred_element_type=jnp.float32,
            )
            taken.append(total[0:1])
        nothing = jnp.zeros((3, LEAF), jnp.float32)
        flux_sums[leaf] = flux_sums[leaf] - jnp.concatenate(taken + [nothing], axis=0)
        return carry

    lax.fori_loop(0, homes, flux_home, 0)
    for k in range(homes + 1):
        own_out[k] = flux_sums[own_first + k]
        own_out[k, 5:6, :] = finished[own_first + k, 38:39, :]
    for k in range(homes + 2):
        above_out[k] = flux_sums[above_first + k]


def pair_sums(tables, counts, windows, slabs, subs):
    homes = counts.shape[0] // subs
    leaves = LEVELS * WIN
    return pl.pallas_call(
        functools.partial(pair_kernel, slabs, subs),
        out_shape=(
            jax.ShapeDtypeStruct((homes + 1, 8, LEAF), jnp.float32),
            jax.ShapeDtypeStruct((homes + 2, 8, LEAF), jnp.float32),
        ),
        in_specs=[SMEM] * 2 + [VMEM] * 4,
        out_specs=(VMEM, VMEM),
        scratch_shapes=[
            pltpu.VMEM((leaves, 8, LEAF), jnp.float32),
            pltpu.VMEM((leaves, 40, LEAF), jnp.float32),
            pltpu.VMEM((len(FLUX_ROWS), LEAF // 8, 8, LEAF), jnp.float32),
            pltpu.VMEM((len(FLUX_ROWS), 8, LEAF), jnp.float32),
            pltpu.VMEM((5, LEAF // 8, 8, LEAF), jnp.float32),
            pltpu.VMEM((leaves, 8, LEAF), jnp.float32),
        ],
        name="pair_sums",
    )(tables, counts, *windows)


def collect_kernel(
    slabs, subs, own, above, all_own, all_below, up_sem, ring_send, ring_recv, core_send, core_recv
):
    slab = lax.axis_index("slab")
    sub = lax.axis_index("sub")
    chips = subs // 2
    chip, core = sub // 2, lax.rem(sub, 2)
    partner = 1 - core
    ahead, behind = around(chip + 1, chips), around(chip - 1, chips)
    right_hops = chips // 2
    left_hops = chips - 1 - right_hops
    barrier = pltpu.get_barrier_semaphore()
    for peer in (
        (around(slab + 1, slabs), sub),
        (around(slab - 1, slabs), sub),
        (slab, 2 * ahead + core),
        (slab, 2 * behind + core),
        (slab, 2 * chip + partner),
    ):
        pl.semaphore_signal(barrier, inc=1, device_id=peer, device_id_type=MESH)
    pl.semaphore_wait(barrier, 5)

    upward = pltpu.make_async_remote_copy(
        src_ref=above,
        dst_ref=all_below.at[sub],
        send_sem=up_sem.at[0],
        recv_sem=up_sem.at[1],
        device_id=(around(slab + 1, slabs), sub),
        device_id_type=MESH,
    )
    upward.start()
    mine = pltpu.make_async_copy(own, all_own.at[sub], up_sem.at[2])
    mine.start()

    def ring(which, source, buffer, owner_chip, hop, to_right):
        slot = 2 * owner_chip + core
        place = (hop - 1) if to_right else (right_hops + hop - 1)
        return pltpu.make_async_remote_copy(
            src_ref=source if source is not None else buffer.at[slot],
            dst_ref=buffer.at[slot],
            send_sem=ring_send.at[which, place],
            recv_sem=ring_recv.at[which, place],
            device_id=(slab, 2 * (ahead if to_right else behind) + core),
            device_id_type=MESH,
        )

    def across(which, source, buffer, owner_chip, place):
        slot = 2 * owner_chip + core
        return pltpu.make_async_remote_copy(
            src_ref=source if source is not None else buffer.at[slot],
            dst_ref=buffer.at[slot],
            send_sem=core_send.at[which, place],
            recv_sem=core_recv.at[which, place],
            device_id=(slab, 2 * chip + partner),
            device_id_type=MESH,
        )

    started, expected = [], []

    def launch(which, source, buffer):
        for to_right, hops in ((True, right_hops), (False, left_hops)):
            if hops > 0:
                one = ring(which, source, buffer, chip, 1, to_right)
                one.start()
                started.append(one)
        one = across(which, source, buffer, chip, 0)
        one.start()
        started.append(one)
        expected.append(one)

    launch(0, own, all_own)
    upward.wait()
    launch(1, None, all_below)
    mine.wait()
    for hop in range(1, right_hops + 1):
        for which, buffer in ((0, all_own), (1, all_below)):
            for to_right, hops in ((True, right_hops), (False, left_hops)):
                if hop > hops:
                    continue
                owner = around(chip - hop, chips) if to_right else around(chip + hop, chips)
                ring(which, None, buffer, owner, hop, to_right).wait_recv()
                if hop < hops:
                    one = ring(which, None, buffer, owner, hop + 1, to_right)
                    one.start()
                    started.append(one)
                place = hop if to_right else right_hops + hop
                one = across(which, None, buffer, owner, place)
                one.start()
                started.append(one)
                expected.append(one)
    for one in expected:
        one.wait_recv()
    for one in started:
        one.wait_send()


def collect_sums(own, above, slabs, subs):
    chips = subs // 2
    return pl.pallas_call(
        functools.partial(collect_kernel, slabs, subs),
        out_shape=(
            jax.ShapeDtypeStruct((subs,) + own.shape, jnp.float32),
            jax.ShapeDtypeStruct((subs,) + above.shape, jnp.float32),
        ),
        in_specs=[VMEM, VMEM],
        out_specs=(VMEM, VMEM),
        scratch_shapes=[
            pltpu.SemaphoreType.DMA((3,)),
            pltpu.SemaphoreType.DMA((2, chips)),
            pltpu.SemaphoreType.DMA((2, chips)),
            pltpu.SemaphoreType.DMA((2, chips)),
            pltpu.SemaphoreType.DMA((2, chips)),
        ],
        compiler_params=pltpu.CompilerParams(collective_id=2, has_side_effects=True),
        name="collect_sums",
    )(own, above)


def total_kernel(subs, tables, all_own, all_below, out):
    homes = all_own.shape[1] - 1
    slab_leaves = subs * homes

    def most(k, value):
        return jnp.maximum(value, tables[k, 2 * homes * KINDS])

    shear = lax.fori_loop(0, 4 * subs, most, jnp.int32(0))
    shear = jnp.where(lax.axis_index("slab") == 0, shear, 0)

    def one(column, carry):
        device, place = column // homes, lax.rem(column, homes)
        mine = all_own[device, place]
        before = all_own[lax.rem(device + subs - 1, subs), homes]
        total = mine + jnp.where(place == 0, 1.0, 0.0).astype(jnp.float32) * before
        source = lax.rem(column - shear + slab_leaves, slab_leaves)
        device, place = source // homes, lax.rem(source, homes)
        total = total + all_below[device, place + 1]
        nearer = all_below[lax.rem(device + subs - 1, subs), homes + 1]
        later = all_below[lax.rem(device + 1, subs), 0]
        total = total + jnp.where(place == 0, 1.0, 0.0).astype(jnp.float32) * nearer
        total = total + jnp.where(place == homes - 1, 1.0, 0.0).astype(jnp.float32) * later
        start = pl.multiple_of(column * LEAF, LEAF)
        out[:, pl.ds(start, LEAF)] = total[0:5] * mine[5:6]
        return carry

    lax.fori_loop(0, slab_leaves, one, 0)


def total_rates(tables, all_own, all_below, subs):
    homes = all_own.shape[1] - 1
    return pl.pallas_call(
        functools.partial(total_kernel, subs),
        out_shape=jax.ShapeDtypeStruct((5, subs * homes * LEAF), jnp.float32),
        in_specs=[SMEM, VMEM, VMEM],
        out_specs=VMEM,
        name="total_rates",
    )(tables, all_own, all_below)


def shards(slabs, subs, positions, velocity, density, pressure, counts, pair_list):
    slab_leaves = counts.shape[0]
    slab = lax.axis_index("slab")
    row = table_row(pair_list, slab, slabs, slab_leaves, slab_leaves // subs)
    tables, own, below, above, beyond = exchange(
        row,
        counts,
        positions,
        velocity,
        density.reshape(slab_leaves, LEAF),
        pressure.reshape(slab_leaves, LEAF),
        slabs,
        subs,
    )
    tables = tables.reshape(4 * subs, LEAF)
    own_part, above_part = pair_sums(tables, counts, (below, own, above, beyond), slabs, subs)
    all_own, all_below = collect_sums(own_part, above_part, slabs, subs)
    return total_rates(tables, all_own, all_below, subs)


def solution(mesh):
    placed = (
        P(None, "slab"),
        P(None, "slab"),
        P("slab"),
        P("slab"),
        P("slab"),
        P(None, ("slab", "sub")),
    )
    return jax.shard_map(
        functools.partial(shards, mesh.shape["slab"], mesh.shape["sub"]),
        mesh=mesh,
        in_specs=placed,
        out_specs=P(None, "slab"),
        check_vma=False,
    )
```

time: 158 us -> 123 us (0.78)
  Pallas kernels: 153 us -> 123 us
  other arithmetic: 4.63 us -> 0.66 us
  local copies, waits for them, and re-layouts: 2.72 us -> 0.68 us
    pallas_call x1, Pallas kernels: 73.5 us -> 52.4 us  [pair_sums(): pl.pallas_call(functools.partial(pair_kernel, slabs, subs), out_shape=(ja...]
    pallas_call x3 -> x1, Pallas kernels: 36.5 us -> 29.6 us  [exchange(): pl.pallas_call(functools.partial(exchange_kernel, slabs, subs), out_shape...]
    pallas_call x1, Pallas kernels: 36.8 us -> 34.5 us  [collect_sums(): pl.pallas_call(functools.partial(collect_kernel, slabs, subs), out_shape=...]
    reshape x4 -> x0, local copies, waits for them, and re-layouts: 1.97 us -> none  [the longest x2 1.37 us: pair_tables(): return (shear, number.reshape(-1), moved.reshape(-1))]
    reduce_max x1, other arithmetic: 1.71 us -> 0.1 us  [table_row(): jnp.max(moved + shears, axis=1)]
where the time goes in v2:
time: 123 us; the launch traced here: 124 us
  Pallas kernels  123 us (100%)
    pallas_call x1, Pallas kernels, pair_sums(): pl.pallas_call(functools.partial(pair_kernel, slabs, subs), out_shape=(ja...  52.4 us
    pallas_call x1, Pallas kernels, collect_sums(): pl.pallas_call(functools.partial(collect_kernel, slabs, subs), out_shape=...  34.5 us
    pallas_call x1, Pallas kernels, exchange(): pl.pallas_call(functools.partial(exchange_kernel, slabs, subs), out_shape...  29.6 us
    pallas_call x1, Pallas kernels, total_rates(): pl.pallas_call(functools.partial(total_kernel, subs), out_shape=jax.Shape...  6.25 us

profile of v2, /device:TPU:1, one launch (start us, length us, event | category | flops | bytes accessed | tf_op | source)
XLA Modules:
  0.0 124.2 jit_solution(6937466241490286616)
XLA Ops:
  0.0 0.0 copy-start
  0.0 0.7 copy-done
  0.7 0.1 fusion
  0.8 0.5 add_bitcast_fusion.row_ref
  1.4 29.6 %exchange.1 = (s32[64,1,128]{2,1,0:T(1,128)}, f32[12,8,128]{2,1,0:T(8,128)}, f32[12,8,128]{2,1,0:T(8,128)}, f32[12,8,128]{2,1,0:T(8,128)}, f32[12,8,128]{2,1,0:T(8,128)}) custom-call(s32[1,1,128]{2,1,0:T(1,128)} %add_bitcast_fusion.row_ref, s32[128]{0:T(128)} %counts.3, f32[3,16384]{1,0:T(4,128)} %positions.1, f32[3,16384]{1,0:T(4,128)} %velocity.1, ...), custom_call_target="tpu_custom_call" | custom-call | tf_op jit(solution)/shard_map/exchange/pallas_call | solution.py:190
  31.0 52.4 %pair_sums.1 = (f32[9,8,128]{2,1,0:T(8,128)}, f32[10,8,128]{2,1,0:T(8,128)}) custom-call(s32[64,128]{1,0:T(8,128)} %bitcast.11, s32[128]{0:T(128)} %counts.3, f32[12,8,128]{2,1,0:T(8,128)} %get-tuple-element.15.below, f32[12,8,128]{2,1,0:T(8,128)} %get-tuple-element.16.own, f32[12,8,128]{2,1,0:T(8,128)} %get-tuple-element.17.above, ...), custom_call_target="tpu_custom_call" | custom-call | tf_op jit(solution)/shard_map/pair_sums/pallas_call | solution.py:582
  83.4 34.5 %collect_sums.1 = (f32[16,9,8,128]{3,2,1,0:T(8,128)}, f32[16,10,8,128]{3,2,1,0:T(8,128)}) custom-call(f32[9,8,128]{2,1,0:T(8,128)} %get-tuple-element.19.own, f32[10,8,128]{2,1,0:T(8,128)} %get-tuple-element.20.above), custom_call_target="tpu_custom_call" | custom-call | tf_op jit(solution)/shard_map/collect_sums/pallas_call | solution.py:700
  117.9 6.3 %total_rates.1 = f32[5,16384]{1,0:T(8,128)} custom-call(s32[64,128]{1,0:T(8,128)} %bitcast.12, f32[16,9,8,128]{3,2,1,0:T(8,128)} %get-tuple-element.21.all_own, f32[16,10,8,128]{3,2,1,0:T(8,128)} %get-tuple-element.22.all_below), custom_call_target="tpu_custom_call" | custom-call | tf_op jit(solution)/shard_map/total_rates/pallas_call | solution.py:751
  (4 shorter events, 0.0 us)
Async XLA Ops:
  0.0 0.7 copy-start

commit v3 on v2

--- a/solution.py
+++ b/solution.py
@@ -297,65 +297,70 @@
     slope_y = ixy * mx + iyy * my + iyz * mz
     slope_z = ixz * mx + iyz * my + izz * mz
     scale = (KERNEL_NORM * SUPPORT) * inverse * inverse
-    return jnp.concatenate(
-        [
-            entries,
-            slope_x,
-            slope_y,
-            slope_z,
-            ixx * scale,
-            ixy * scale,
-            ixz * scale,
-            iyy * scale,
-            iyz * scale,
-            izz * scale,
-            number,
-            number,
-        ],
-        axis=0,
-    )
-
-
-FLUX_ROWS = (
-    tuple(range(8))
-    + tuple(8 * k + 11 + q for q in range(5) for k in range(3))
-    + tuple(range(32, 38))
-)
-
-
-def flux_terms(near, far, weight):
-    d = [far(k) - near(k) for k in range(3)]
-    smooth = weights(d[0] * d[0] + d[1] * d[1] + d[2] * d[2])
-    mxx, mxy, mxz, myy, myz, mzz = [near(23 + k) + far(23 + k) for k in range(6)]
-    area = [
-        smooth * (mxx * d[0] + mxy * d[1] + mxz * d[2]),
-        smooth * (mxy * d[0] + myy * d[1] + myz * d[2]),
-        smooth * (mxz * d[0] + myz * d[1] + mzz * d[2]),
-    ]
+    inverse_rows = [k * scale for k in (ixx, ixy, ixz, iyy, iyz, izz)]
+    return number, (slope_x, slope_y, slope_z), inverse_rows
+
+
+def flux_base(entries, row, last):
+    return jnp.where(row < 6, entries, jnp.where(row == 6, 1.0, last))
+
+
+def flux_coefficients(entries, slopes, inverse_rows, row):
+    x, y, z = entries[0:1], entries[1:2], entries[2:3]
+    constant = entries - slopes[0] * x - slopes[1] * y - slopes[2] * z
+    planes = []
+    for q in range(5):
+        at = slice(3 + q, 4 + q)
+        plane = jnp.where(
+            row == 0,
+            slopes[0][at],
+            jnp.where(
+                row == 1,
+                slopes[1][at],
+                jnp.where(row == 2, slopes[2][at], jnp.where(row == 6, constant[at], 0.0)),
+            ),
+        )
+        if q < 3:
+            plane = jnp.where(row == 3 + q, -1.0, plane)
+        planes.append(plane)
+    ixx, ixy, ixz, iyy, iyz, izz = inverse_rows
+    for a, b, c in ((ixx, ixy, ixz), (ixy, iyy, iyz), (ixz, iyz, izz)):
+        rest = -(a * x + b * y + c * z)
+        planes.append(
+            jnp.where(
+                row == 0,
+                a,
+                jnp.where(row == 1, b, jnp.where(row == 2, c, jnp.where(row == 6, rest, 0.0))),
+            )
+        )
+    return planes
+
+
+PLANES = 14
+
+
+def flux_terms(plane, near, far, weight):
+    smooth = weights(plane(13))
+    area = [smooth * plane(10 + k) for k in range(3)]
     area_sq = area[0] * area[0] + area[1] * area[1] + area[2] * area[2]
     root = lax.rsqrt(jnp.maximum(area_sq, TINY))
     size = area_sq * root * weight
     root = jnp.minimum(root, 1.0 / AREA_FLOOR)
     normal = [area[k] * root for k in range(3)]
-
-    def slope(side, q):
-        return side(8 + 3 * q) * d[0] + side(9 + 3 * q) * d[1] + side(10 + 3 * q) * d[2]
-
     left_vel, right_vel, face = [], [], []
     for q in range(3):
-        a, b = near(3 + q), far(3 + q)
+        a, b = near(q), far(q)
         face.append(a + b)
-        gap = b - a
-        high = jnp.abs(gap)
+        high = jnp.abs(b - a)
         low = -high
-        left_vel.append(jnp.minimum(jnp.maximum(slope(near, q) - gap, low), high))
-        right_vel.append(jnp.minimum(jnp.maximum(gap - slope(far, q), low), high))
+        left_vel.append(jnp.minimum(jnp.maximum(plane(q), low), high))
+        right_vel.append(jnp.minimum(jnp.maximum(plane(5 + q), low), high))
     states = []
     for q in (3, 4):
-        a, b = near(3 + q), far(3 + q)
+        a, b = near(q), far(q)
         low, high = jnp.minimum(a, b), jnp.maximum(a, b)
-        states.append(jnp.minimum(jnp.maximum(a + slope(near, q), low), high))
-        states.append(jnp.minimum(jnp.maximum(b - slope(far, q), low), high))
+        states.append(jnp.minimum(jnp.maximum(plane(q), low), high))
+        states.append(jnp.minimum(jnp.maximum(plane(5 + q), low), high))
     left_rho, right_rho, left_p, right_p = states
     left_un = left_vel[0] * normal[0] + left_vel[1] * normal[1] + left_vel[2] * normal[2]
     right_un = right_vel[0] * normal[0] + right_vel[1] * normal[1] + right_vel[2] * normal[2]
@@ -404,11 +409,17 @@
     own_out,
     above_out,
     store,
-    finished,
+    numbers,
+    coefficients,
+    right_parts,
+    left_parts,
     near_rows,
     far_rows,
+    planes_one,
+    planes_two,
     row_sums,
     flux_sums,
+    tiles,
 ):
     slab = lax.axis_index("slab")
     sub = lax.axis_index("sub")
@@ -498,80 +509,149 @@
                 preferred_element_type=jnp.float32,
             )
             sums = part if sums is None else sums + part
-        finished[leaf] = finish(moment_rows(sums, mine), mine)
-        finished[leaf, 0:8] = mine * halves
+        number, slopes, inverse_rows = finish(moment_rows(sums, mine), mine)
+        halved = mine * halves
+        numbers[leaf] = jnp.broadcast_to(number, (8, LEAF))
+        pad = jnp.zeros((16, LEAF), jnp.bfloat16)
+        for k, plane in enumerate(flux_coefficients(halved, slopes, inverse_rows, row)):
+            coefficients[leaf, k] = plane
+            part = right_stack(plane if k < 5 else -plane)
+            right_parts[leaf, k] = jnp.concatenate([part, pad], axis=0)
         return carry
 
     lax.fori_loop(0, 2 * homes + 3, finish_one, 0)
+
+    blank = jnp.zeros((LEAF, LEAF), jnp.float32)
+
+    def turned_left(full, first):
+        stack = left_stack(full).astype(jnp.float32)
+        parts = ([blank[:first]] if first else []) + [stack, blank[: LEAF - 48 - first]]
+        return jnp.transpose(jnp.concatenate(parts, axis=0)).astype(jnp.bfloat16)
+
+    def prepare_home(place, carry):
+        leaf = own_first + place
+        mine = store[leaf] * halves
+        for k in range(8):
+            left_parts[place, k] = turned_left(coefficients[leaf, k], 0)
+        distance = jnp.where(
+            row < 3,
+            -2.0 * mine,
+            jnp.where(row < 6, 0.0, jnp.where(row == 6, length_sq(mine), 1.0)),
+        )
+        left_parts[place, 8] = turned_left(distance, 0)
+        turned = jnp.transpose(mine)
+        for k in range(5):
+            near_rows[place, k] = jnp.broadcast_to(
+                turned[:, 3 + k : 4 + k], (LEAF, LEAF)
+            ).reshape(LEAF // 8, 8, LEAF)
+        row_sums[place] = jnp.zeros((5, LEAF // 8, 8, LEAF), jnp.float32)
+        return carry
+
+    lax.fori_loop(0, homes, prepare_home, 0)
+
+    own_row = 2 * subs + sub
+
+    def clear(k, carry):
+        tiles[k] = 0
+        return carry
+
+    lax.fori_loop(0, table_size + 8, clear, 0)
+
+    def list_tile(entry, filled):
+        tiles[filled] = entry
+        return filled + jnp.where(tables[own_row, entry] > 0, 1, 0)
+
+    filled = lax.fori_loop(0, table_size, list_tile, jnp.int32(0))
+
+    def tile_facts(index):
+        entry = tiles[index]
+        place = entry // KINDS
+        kind = entry - place * KINDS
+        number, away, gap_x, gap_y, gap_v = pair_facts(home_facts(1, place), kind)
+        number = jnp.where(index < filled, number, 0).astype(jnp.float32)
+        scale = number * jnp.where(kind == 0, 0.5, 1.0).astype(jnp.float32)
+        leaf = own_first + place
+        return place, leaf, leaf + away, gap_x, gap_y, 0.5 * gap_v, scale
+
+    def lay_planes(index, planes):
+        place, leaf, other, gap_x, gap_y, gap_v, _ = tile_facts(index)
+        theirs = displaced(store[other] * halves, row, gap_x, gap_y, gap_v)
+        base = right_stack(flux_base(theirs, row, length_sq(theirs)))
+        base = jnp.concatenate([base, jnp.zeros((16, LEAF), jnp.bfloat16)], axis=0)
+        mine = store[leaf] * halves - jnp.where(
+            row == 0, gap_x, jnp.where(row == 1, gap_y, jnp.where(row == 4, gap_v, 0.0))
+        )
+        mine = turned_left(flux_base(mine, row, 0.0), 64)
+        for k in range(8):
+            right = jnp.concatenate([base, right_parts[other, k]], axis=0)
+            left = left_parts[place, k]
+            if k < 5:
+                parts = [left, mine] + ([left_parts[place, 8]] if k == 0 else [])
+                targets = [k, 5 + k] + ([13] if k == 0 else [])
+            else:
+                parts = [left + mine]
+                targets = [5 + k]
+            for part, target in zip(parts, targets):
+                planes[target] = lax.dot_general(
+                    part,
+                    right,
+                    (((1,), (0,)), ((), ())),
+                    preferred_element_type=jnp.float32,
+                ).reshape(LEAF // 8, 8, LEAF)
+
+    def add_fluxes(index, planes, far_rows):
+        place, _, other, gap_x, gap_y, gap_v, scale = tile_facts(index)
+        theirs = displaced(store[other] * halves, row, gap_x, gap_y, gap_v)
+        for k in range(5):
+            far_rows[k] = jnp.broadcast_to(theirs[3 + k : 4 + k], (8, LEAF))
+        totals = [None] * 5
+        for first in range(0, LEAF // 8, BLOCK):
+            terms = flux_terms(
+                lambda k: planes[k, first : first + BLOCK],
+                lambda k: near_rows[place, k, first : first + BLOCK],
+                lambda k: far_rows[k][None],
+                scale,
+            )
+            for k in range(5):
+                row_sums[place, k, first : first + BLOCK] += terms[k]
+                part = jnp.sum(terms[k], axis=0)
+                totals[k] = part if totals[k] is None else totals[k] + part
+        added = [jnp.sum(part, axis=0, keepdims=True) for part in totals]
+        nothing = jnp.zeros((3, LEAF), jnp.float32)
+        flux_sums[other] = flux_sums[other] + jnp.concatenate(added + [nothing], axis=0)
+
+    lay_planes(0, planes_one)
+
+    def two_tiles(step, carry):
+        lay_planes(2 * step + 1, planes_two)
+        add_fluxes(2 * step, planes_one, far_rows.at[0])
+        lay_planes(2 * step + 2, planes_one)
+        add_fluxes(2 * step + 1, planes_two, far_rows.at[1])
+        return carry
+
+    lax.fori_loop(0, (filled + 1) // 2, two_tiles, 0)
     ones = jnp.ones((8, LEAF), jnp.float32)
 
-    def flux_home(place, carry):
-        leaf = own_first + place
-        facts = home_facts(1, place)
-        turned = jnp.transpose(finished[leaf])
-        for k, source in enumerate(FLUX_ROWS):
-            near_rows[k] = jnp.broadcast_to(turned[:, source : source + 1], (LEAF, LEAF)).reshape(
-                LEAF // 8, 8, LEAF
-            )
-        row_sums[...] = jnp.zeros_like(row_sums)
-        steps = (counts[facts[1]] + 8 * BLOCK - 1) // (8 * BLOCK)
-
-        def one(kind, carry):
-            number, away, gap_x, gap_y, gap_v = pair_facts(facts, kind)
-            other = leaf + away
-            scale = number.astype(jnp.float32) * jnp.where(kind == 0, 0.5, 1.0).astype(jnp.float32)
-
-            @pl.when(number > 0)
-            def _():
-                theirs = finished[other]
-                head = displaced(theirs[0:8], row, gap_x, gap_y, 0.5 * gap_v)
-                for k, source in enumerate(FLUX_ROWS):
-                    part = head if source < 8 else theirs
-                    far_rows[k] = jnp.broadcast_to(part[source : source + 1], (8, LEAF))
-
-                def step(group, sums):
-                    first = group * BLOCK
-
-                    def near(k):
-                        return near_rows[k, pl.ds(first, BLOCK)]
-
-                    def far(k):
-                        return far_rows[k][None]
-
-                    terms = flux_terms(near, far, scale)
-                    totals = []
-                    for k in range(5):
-                        row_sums[k, pl.ds(first, BLOCK)] += terms[k]
-                        totals.append(sums[k] + jnp.sum(terms[k], axis=0))
-                    return tuple(totals)
-
-                empty = jnp.zeros((8, LEAF), jnp.float32)
-                sums = lax.fori_loop(0, steps, step, (empty,) * 5)
-                added = [jnp.sum(part, axis=0, keepdims=True) for part in sums]
-                nothing = jnp.zeros((3, LEAF), jnp.float32)
-                flux_sums[other] = flux_sums[other] + jnp.concatenate(added + [nothing], axis=0)
-
-            return carry
-
-        lax.fori_loop(0, KINDS, one, 0)
+    def close_home(place, carry):
         taken = []
         for k in range(5):
             total = lax.dot_general(
                 ones,
-                row_sums[k].reshape(LEAF, LEAF),
+                row_sums[place, k].reshape(LEAF, LEAF),
                 (((1,), (1,)), ((), ())),
                 precision=HIGHEST,
                 preferred_element_type=jnp.float32,
             )
             taken.append(total[0:1])
         nothing = jnp.zeros((3, LEAF), jnp.float32)
+        leaf = own_first + place
         flux_sums[leaf] = flux_sums[leaf] - jnp.concatenate(taken + [nothing], axis=0)
         return carry
 
-    lax.fori_loop(0, homes, flux_home, 0)
+    lax.fori_loop(0, homes, close_home, 0)
     for k in range(homes + 1):
         own_out[k] = flux_sums[own_first + k]
-        own_out[k, 5:6, :] = finished[own_first + k, 38:39, :]
+        own_out[k, 5:6, :] = numbers[own_first + k, 0:1, :]
     for k in range(homes + 2):
         above_out[k] = flux_sums[above_first + k]
 
@@ -589,11 +669,17 @@
         out_specs=(VMEM, VMEM),
         scratch_shapes=[
             pltpu.VMEM((leaves, 8, LEAF), jnp.float32),
-            pltpu.VMEM((leaves, 40, LEAF), jnp.float32),
-            pltpu.VMEM((len(FLUX_ROWS), LEAF // 8, 8, LEAF), jnp.float32),
-            pltpu.VMEM((len(FLUX_ROWS), 8, LEAF), jnp.float32),
-            pltpu.VMEM((5, LEAF // 8, 8, LEAF), jnp.float32),
             pltpu.VMEM((leaves, 8, LEAF), jnp.float32),
+            pltpu.VMEM((leaves, 8, 8, LEAF), jnp.float32),
+            pltpu.VMEM((leaves, 8, 64, LEAF), jnp.bfloat16),
+            pltpu.VMEM((homes, 9, LEAF, LEAF), jnp.bfloat16),
+            pltpu.VMEM((homes, 5, LEAF // 8, 8, LEAF), jnp.float32),
+            pltpu.VMEM((2, 5, 8, LEAF), jnp.float32),
+            pltpu.VMEM((PLANES, LEAF // 8, 8, LEAF), jnp.float32),
+            pltpu.VMEM((PLANES, LEAF // 8, 8, LEAF), jnp.float32),
+            pltpu.VMEM((homes, 5, LEAF // 8, 8, LEAF), jnp.float32),
+            pltpu.VMEM((leaves, 8, LEAF), jnp.float32),
+            pltpu.SMEM((homes * KINDS + 8,), jnp.int32),
         ],
         name="pair_sums",
     )(tables, counts, *windows)
@@ -743,7 +829,7 @@
         out[:, pl.ds(start, LEAF)] = total[0:5] * mine[5:6]
         return carry
 
-    lax.fori_loop(0, slab_leaves, one, 0)
+    lax.fori_loop(0, slab_leaves, one, 0, unroll=8)
 
 
 def total_rates(tables, all_own, all_below, subs):

time: 123 us -> 111 us (0.902); the launches traced: 124 us -> 111 us
  Pallas kernels: 123 us -> 109 us
    pallas_call x1, Pallas kernels: 34.5 us -> 23 us  [collect_sums(): pl.pallas_call(functools.partial(collect_kernel, slabs, subs), out_shape=...]
    pallas_call x1, Pallas kernels: 52.4 us -> 51 us  [pair_sums(): pl.pallas_call(functools.partial(pair_kernel, slabs, subs), out_shape=(ja...]
where the time goes in v3:
time: 111 us
  Pallas kernels  109 us (98%)
    pallas_call x1, Pallas kernels, pair_sums(): pl.pallas_call(functools.partial(pair_kernel, slabs, subs), out_shape=(ja...  51 us
    pallas_call x1, Pallas kernels, exchange(): pl.pallas_call(functools.partial(exchange_kernel, slabs, subs), out_shape...  29.6 us
    pallas_call x1, Pallas kernels, collect_sums(): pl.pallas_call(functools.partial(collect_kernel, slabs, subs), out_shape=...  23 us
    pallas_call x1, Pallas kernels, total_rates(): pl.pallas_call(functools.partial(total_kernel, subs), out_shape=jax.Shape...  5.63 us

profile of v3, /device:TPU:1, one launch (start us, length us, event | category | flops | bytes accessed | tf_op | source)
XLA Modules:
  0.0 110.7 jit_solution(13409802739597149868)
XLA Ops:
  0.0 0.0 copy-start
  0.0 0.7 copy-done
  0.7 0.1 fusion
  0.8 0.5 add_bitcast_fusion.row_ref
  1.4 29.6 %exchange.1 = (s32[64,1,128]{2,1,0:T(1,128)}, f32[12,8,128]{2,1,0:T(8,128)}, f32[12,8,128]{2,1,0:T(8,128)}, f32[12,8,128]{2,1,0:T(8,128)}, f32[12,8,128]{2,1,0:T(8,128)}) custom-call(s32[1,1,128]{2,1,0:T(1,128)} %add_bitcast_fusion.row_ref, s32[128]{0:T(128)} %counts.3, f32[3,16384]{1,0:T(4,128)} %positions.1, f32[3,16384]{1,0:T(4,128)} %velocity.1, ...), custom_call_target="tpu_custom_call" | custom-call | tf_op jit(solution)/shard_map/exchange/pallas_call | solution.py:190
  31.0 51.0 %pair_sums.1 = (f32[9,8,128]{2,1,0:T(8,128)}, f32[10,8,128]{2,1,0:T(8,128)}) custom-call(s32[64,128]{1,0:T(8,128)} %bitcast.11, s32[128]{0:T(128)} %counts.3, f32[12,8,128]{2,1,0:T(8,128)} %get-tuple-element.15.below, f32[12,8,128]{2,1,0:T(8,128)} %get-tuple-element.16.own, f32[12,8,128]{2,1,0:T(8,128)} %get-tuple-element.17.above, ...), custom_call_target="tpu_custom_call" | custom-call | tf_op jit(solution)/shard_map/pair_sums/pallas_call | solution.py:662
  82.1 23.0 %collect_sums.1 = (f32[16,9,8,128]{3,2,1,0:T(8,128)}, f32[16,10,8,128]{3,2,1,0:T(8,128)}) custom-call(f32[9,8,128]{2,1,0:T(8,128)} %get-tuple-element.19.own, f32[10,8,128]{2,1,0:T(8,128)} %get-tuple-element.20.above), custom_call_target="tpu_custom_call" | custom-call | tf_op jit(solution)/shard_map/collect_sums/pallas_call | solution.py:786
  105.1 5.6 %total_rates.1 = f32[5,16384]{1,0:T(8,128)} custom-call(s32[64,128]{1,0:T(8,128)} %bitcast.12, f32[16,9,8,128]{3,2,1,0:T(8,128)} %get-tuple-element.21.all_own, f32[16,10,8,128]{3,2,1,0:T(8,128)} %get-tuple-element.22.all_below), custom_call_target="tpu_custom_call" | custom-call | tf_op jit(solution)/shard_map/total_rates/pallas_call | solution.py:837
  (4 shorter events, 0.0 us)
Async XLA Ops:
  0.0 0.7 copy-start

commit v4 on v3

--- a/solution.py
+++ b/solution.py
@@ -14,7 +14,7 @@
 LEVELS = 4
 GAMMA = 5.0 / 3.0
 SUPPORT = 1.5
-KERNEL_NORM = 21.0 / (2.0 * math.pi * SUPPORT**3)
+KERNEL_NORM = 4.0 * 21.0 / (2.0 * math.pi * SUPPORT**3)
 MOMENT_REG = 0.05
 AREA_FLOOR = 0.0001
 FAR_AWAY = 1.0e6
@@ -221,35 +221,31 @@
     )
 
 
-def features(entries, scale):
+def features(entries, scale, row):
     scaled = scale * entries
     full = jnp.concatenate(
         [
             scaled,
             entries[0:1] * scaled,
-            entries[1:2] * scaled,
+            jnp.where(row == 0, scale, entries[1:2] * scaled),
             entries[2:3] * scaled,
-            jnp.full_like(entries, scale),
         ],
         axis=0,
     )
     return jnp.concatenate(three_parts(full), axis=0).astype(jnp.bfloat16)
 
 
-def moment_rows(sums, entries):
-    sums = sums[0:40] + sums[40:80] + sums[80:120]
-    plain, total = sums[0:8], sums[32:33]
+def moment_rows(sums, entries, row):
+    sums = KERNEL_NORM * (sums[0:32] + sums[32:64] + sums[64:96])
+    plain, total = sums[0:8], sums[16:17]
+    times = (sums[8:16], jnp.where(row == 0, sums[9:10], sums[16:24]), sums[24:32])
     parts = []
     for k in range(3):
         own = entries[k : k + 1]
         parts.append(
-            sums[8 * k + 8 : 8 * k + 16]
-            - own * plain
-            - entries * sums[k : k + 1]
-            + own * (entries * total)
-        )
-    parts.append(sums[32:40])
-    return KERNEL_NORM * jnp.concatenate(parts, axis=0)
+            times[k] - own * plain - entries * sums[k : k + 1] + own * (entries * total)
+        )
+    return parts, total
 
 
 def displaced(entries, row, gap_x, gap_y, gap_v):
@@ -268,20 +264,21 @@
     dist_sq = jnp.maximum(dist_sq, TINY)
     inside = jnp.maximum(1.0 - dist_sq * lax.rsqrt(dist_sq), 0.0)
     square = inside * inside
-    return square * square * (5.0 - 4.0 * inside)
-
-
-def finish(sums, entries):
+    return square * square * (1.25 - inside)
+
+
+def finish(parts, total, entries):
     live = (entries[0:1] < DEAD_ABOVE).astype(jnp.float32)
-    number = sums[24:25] + 1.0 - live
+    number = total + 1.0 - live
     inverse = 1.0 / number
     area = inverse * SUPPORT**2
-    xx = sums[0:1] * area + MOMENT_REG
-    xy = sums[1:2] * area
-    xz = sums[2:3] * area
-    yy = sums[9:10] * area + MOMENT_REG
-    yz = sums[10:11] * area
-    zz = sums[18:19] * area + MOMENT_REG
+    mx, my, mz = parts
+    xx = mx[0:1] * area + MOMENT_REG
+    xy = mx[1:2] * area
+    xz = mx[2:3] * area
+    yy = my[1:2] * area + MOMENT_REG
+    yz = my[2:3] * area
+    zz = mz[2:3] * area + MOMENT_REG
     minor_xx = yy * zz - yz * yz
     minor_xy = xz * yz - xy * zz
     minor_xz = xy * yz - xz * yy
@@ -292,7 +289,7 @@
     ixx, ixy, ixz = minor_xx * unit, minor_xy * unit, minor_xz * unit
     iyy, iyz, izz = minor_yy * unit, minor_yz * unit, minor_zz * unit
     half = 0.5 * area
-    mx, my, mz = sums[0:8] * half, sums[8:16] * half, sums[16:24] * half
+    mx, my, mz = mx * half, my * half, mz * half
     slope_x = ixx * mx + ixy * my + ixz * mz
     slope_y = ixy * mx + iyy * my + iyz * mz
     slope_z = ixz * mx + iyz * my + izz * mz
@@ -420,6 +417,7 @@
     row_sums,
     flux_sums,
     tiles,
+    tile_gaps,
 ):
     slab = lax.axis_index("slab")
     sub = lax.axis_index("sub")
@@ -481,35 +479,39 @@
         pairs.append((home_facts(level, place - 1), 1, -1))
         pairs += [(home_facts(level - 1, place + 3 - kind), kind, -1) for kind in (2, 3, 4)]
         sums = None
-        for facts, kind, sign in pairs:
-            number, away, gap_x, gap_y, gap_v = pair_facts(facts, kind)
-            theirs = displaced(
-                store[leaf + sign * away], row, sign * gap_x, sign * gap_y, sign * gap_v
-            )
-            right = jnp.where(
-                row < 3,
-                theirs,
-                jnp.where(row == 3, length_sq(theirs), jnp.where(row == 4, 1.0, 0.0)),
-            )
+        for first in range(0, len(pairs), 2):
+            rows, rights = [], []
+            for facts, kind, sign in pairs[first : first + 2]:
+                number, away, gap_x, gap_y, gap_v = pair_facts(facts, kind)
+                theirs = displaced(
+                    store[leaf + sign * away], row, sign * gap_x, sign * gap_y, sign * gap_v
+                )
+                right = jnp.where(
+                    row < 3,
+                    theirs,
+                    jnp.where(row == 3, length_sq(theirs), jnp.where(row == 4, 1.0, 0.0)),
+                )
+                rights.append(right_stack(right))
+                rows.append(features(theirs, number.astype(jnp.float32), row))
             smooth = weights(
                 lax.dot_general(
                     left,
-                    right_stack(right),
+                    jnp.concatenate(rights, axis=1),
                     (((1,), (0,)), ((), ())),
                     preferred_element_type=jnp.float32,
                 )
             )
             high = smooth.astype(jnp.bfloat16)
             low = (smooth - high.astype(jnp.float32)).astype(jnp.bfloat16)
-            rows = features(theirs, number.astype(jnp.float32))
             part = lax.dot_general(
-                jnp.concatenate([rows, rows], axis=1),
+                jnp.concatenate(rows + rows, axis=1),
                 jnp.concatenate([high, low], axis=1),
                 (((1,), (1,)), ((), ())),
                 preferred_element_type=jnp.float32,
             )
             sums = part if sums is None else sums + part
-        number, slopes, inverse_rows = finish(moment_rows(sums, mine), mine)
+        parts, total = moment_rows(sums, mine, row)
+        number, slopes, inverse_rows = finish(parts, total, mine)
         halved = mine * halves
         numbers[leaf] = jnp.broadcast_to(number, (8, LEAF))
         pad = jnp.zeros((16, LEAF), jnp.bfloat16)
@@ -547,31 +549,31 @@
         row_sums[place] = jnp.zeros((5, LEAF // 8, 8, LEAF), jnp.float32)
         return carry
 
-    lax.fori_loop(0, homes, prepare_home, 0)
-
-    own_row = 2 * subs + sub
-
-    def clear(k, carry):
-        tiles[k] = 0
-        return carry
-
-    lax.fori_loop(0, table_size + 8, clear, 0)
+    lax.fori_loop(0, homes, prepare_home, 0, unroll=2)
+
+    def put_tile(index, place, other, gap_x, gap_y, gap_v, scale):
+        tiles[2 * index] = place
+        tiles[2 * index + 1] = other
+        for k, value in enumerate((gap_x, gap_y, gap_v, scale)):
+            tile_gaps[4 * index + k] = value
 
     def list_tile(entry, filled):
-        tiles[filled] = entry
-        return filled + jnp.where(tables[own_row, entry] > 0, 1, 0)
-
-    filled = lax.fori_loop(0, table_size, list_tile, jnp.int32(0))
-
-    def tile_facts(index):
-        entry = tiles[index]
         place = entry // KINDS
         kind = entry - place * KINDS
         number, away, gap_x, gap_y, gap_v = pair_facts(home_facts(1, place), kind)
-        number = jnp.where(index < filled, number, 0).astype(jnp.float32)
-        scale = number * jnp.where(kind == 0, 0.5, 1.0).astype(jnp.float32)
-        leaf = own_first + place
-        return place, leaf, leaf + away, gap_x, gap_y, 0.5 * gap_v, scale
+        scale = number.astype(jnp.float32) * jnp.where(kind == 0, 0.5, 1.0).astype(jnp.float32)
+        put_tile(filled, place, own_first + place + away, gap_x, gap_y, 0.5 * gap_v, scale)
+        return filled + jnp.where(number > 0, 1, 0)
+
+    filled = lax.fori_loop(0, table_size, list_tile, jnp.int32(0))
+    nought = jnp.float32(0.0)
+    for k in range(3):
+        put_tile(filled + k, jnp.int32(0), jnp.int32(own_first), nought, nought, nought, nought)
+
+    def tile_facts(index):
+        place = tiles[2 * index]
+        gaps = [tile_gaps[4 * index + k] for k in range(4)]
+        return (place, own_first + place, tiles[2 * index + 1], *gaps)
 
     def lay_planes(index, planes):
         place, leaf, other, gap_x, gap_y, gap_v, _ = tile_facts(index)
@@ -630,30 +632,29 @@
         return carry
 
     lax.fori_loop(0, (filled + 1) // 2, two_tiles, 0)
-    ones = jnp.ones((8, LEAF), jnp.float32)
-
     def close_home(place, carry):
+        leaf = own_first + place
         taken = []
         for k in range(5):
-            total = lax.dot_general(
-                ones,
-                row_sums[place, k].reshape(LEAF, LEAF),
-                (((1,), (1,)), ((), ())),
-                precision=HIGHEST,
-                preferred_element_type=jnp.float32,
-            )
-            taken.append(total[0:1])
+            turned = jnp.transpose(row_sums[place, k].reshape(LEAF, LEAF))
+            taken.append(jnp.sum(turned, axis=0, keepdims=True))
         nothing = jnp.zeros((3, LEAF), jnp.float32)
-        leaf = own_first + place
         flux_sums[leaf] = flux_sums[leaf] - jnp.concatenate(taken + [nothing], axis=0)
         return carry
 
-    lax.fori_loop(0, homes, close_home, 0)
-    for k in range(homes + 1):
-        own_out[k] = flux_sums[own_first + k]
-        own_out[k, 5:6, :] = numbers[own_first + k, 0:1, :]
-    for k in range(homes + 2):
-        above_out[k] = flux_sums[above_first + k]
+    lax.fori_loop(0, homes, close_home, 0, unroll=2)
+    for out, first, size in (
+        (own_out, own_first, homes + 1),
+        (above_out, above_first, homes + 2),
+    ):
+        out[5 * size :, :] = jnp.zeros((out.shape[0] - 5 * size, LEAF), jnp.float32)
+        for k in range(size):
+            rates = flux_sums[first + k] * numbers[first + k]
+            out[5 * k : 5 * k + 5, :] = rates[0:5]
+
+
+def packed_rows(leaves):
+    return -(-5 * leaves // 8) * 8
 
 
 def pair_sums(tables, counts, windows, slabs, subs):
@@ -662,8 +663,8 @@
     return pl.pallas_call(
         functools.partial(pair_kernel, slabs, subs),
         out_shape=(
-            jax.ShapeDtypeStruct((homes + 1, 8, LEAF), jnp.float32),
-            jax.ShapeDtypeStruct((homes + 2, 8, LEAF), jnp.float32),
+            jax.ShapeDtypeStruct((packed_rows(homes + 1), LEAF), jnp.float32),
+            jax.ShapeDtypeStruct((packed_rows(homes + 2), LEAF), jnp.float32),
         ),
         in_specs=[SMEM] * 2 + [VMEM] * 4,
         out_specs=(VMEM, VMEM),
@@ -679,17 +680,19 @@
             pltpu.VMEM((PLANES, LEAF // 8, 8, LEAF), jnp.float32),
             pltpu.VMEM((homes, 5, LEAF // 8, 8, LEAF), jnp.float32),
             pltpu.VMEM((leaves, 8, LEAF), jnp.float32),
-            pltpu.SMEM((homes * KINDS + 8,), jnp.int32),
+            pltpu.SMEM((2 * homes * KINDS + 8,), jnp.int32),
+            pltpu.SMEM((4 * homes * KINDS + 16,), jnp.float32),
         ],
         name="pair_sums",
     )(tables, counts, *windows)
 
 
 def collect_kernel(
-    slabs, subs, own, above, all_own, all_below, up_sem, ring_send, ring_recv, core_send, core_recv
+    slabs, subs, chunks, own, above, gathered, up_sem, ring_send, ring_recv, core_send, core_recv
 ):
     slab = lax.axis_index("slab")
     sub = lax.axis_index("sub")
+    own_size, above_size = own.shape[0], above.shape[0]
     chips = subs // 2
     chip, core = sub // 2, lax.rem(sub, 2)
     partner = 1 - core
@@ -709,72 +712,89 @@
 
     upward = pltpu.make_async_remote_copy(
         src_ref=above,
-        dst_ref=all_below.at[sub],
+        dst_ref=gathered.at[sub, pl.ds(own_size, above_size)],
         send_sem=up_sem.at[0],
         recv_sem=up_sem.at[1],
         device_id=(around(slab + 1, slabs), sub),
         device_id_type=MESH,
     )
     upward.start()
-    mine = pltpu.make_async_copy(own, all_own.at[sub], up_sem.at[2])
+    mine = pltpu.make_async_copy(own, gathered.at[sub, pl.ds(0, own_size)], up_sem.at[2])
     mine.start()
 
-    def ring(which, source, buffer, owner_chip, hop, to_right):
-        slot = 2 * owner_chip + core
+    def transfer(which, owner_chip, first, peer, send_sem, recv_sem):
+        start, size = chunks[which]
+        target = gathered.at[2 * owner_chip + core, pl.ds(start, size)]
+        source = own.at[pl.ds(start, size)] if first and start < own_size else target
+        return pltpu.make_async_remote_copy(
+            src_ref=source,
+            dst_ref=target,
+            send_sem=send_sem,
+            recv_sem=recv_sem,
+            device_id=(slab, peer),
+            device_id_type=MESH,
+        )
+
+    def ring(which, owner_chip, hop, to_right):
         place = (hop - 1) if to_right else (right_hops + hop - 1)
-        return pltpu.make_async_remote_copy(
-            src_ref=source if source is not None else buffer.at[slot],
-            dst_ref=buffer.at[slot],
-            send_sem=ring_send.at[which, place],
-            recv_sem=ring_recv.at[which, place],
-            device_id=(slab, 2 * (ahead if to_right else behind) + core),
-            device_id_type=MESH,
-        )
-
-    def across(which, source, buffer, owner_chip, place):
-        slot = 2 * owner_chip + core
-        return pltpu.make_async_remote_copy(
-            src_ref=source if source is not None else buffer.at[slot],
-            dst_ref=buffer.at[slot],
-            send_sem=core_send.at[which, place],
-            recv_sem=core_recv.at[which, place],
-            device_id=(slab, 2 * chip + partner),
-            device_id_type=MESH,
+        return transfer(
+            which,
+            owner_chip,
+            hop == 1,
+            2 * (ahead if to_right else behind) + core,
+            ring_send.at[which, place],
+            ring_recv.at[which, place],
+        )
+
+    def across(which, owner_chip, place):
+        return transfer(
+            which,
+            owner_chip,
+            place == 0,
+            2 * chip + partner,
+            core_send.at[which, place],
+            core_recv.at[which, place],
         )
 
     started, expected = [], []
 
-    def launch(which, source, buffer):
+    def launch(which):
         for to_right, hops in ((True, right_hops), (False, left_hops)):
             if hops > 0:
-                one = ring(which, source, buffer, chip, 1, to_right)
+                one = ring(which, chip, 1, to_right)
                 one.start()
                 started.append(one)
-        one = across(which, source, buffer, chip, 0)
+        one = across(which, chip, 0)
         one.start()
         started.append(one)
         expected.append(one)
 
-    launch(0, own, all_own)
+    def forward(which, hop):
+        for to_right, hops in ((True, right_hops), (False, left_hops)):
+            if hop > hops:
+                continue
+            owner = around(chip - hop, chips) if to_right else around(chip + hop, chips)
+            ring(which, owner, hop, to_right).wait_recv()
+            if hop < hops:
+                one = ring(which, owner, hop + 1, to_right)
+                one.start()
+                started.append(one)
+            one = across(which, owner, hop if to_right else right_hops + hop)
+            one.start()
+            started.append(one)
+            expected.append(one)
+
+    early = [k for k, (start, _) in enumerate(chunks) if start < own_size]
+    late = [k for k, (start, _) in enumerate(chunks) if start >= own_size]
+    for which in early:
+        launch(which)
     upward.wait()
-    launch(1, None, all_below)
+    for which in late:
+        launch(which)
     mine.wait()
     for hop in range(1, right_hops + 1):
-        for which, buffer in ((0, all_own), (1, all_below)):
-            for to_right, hops in ((True, right_hops), (False, left_hops)):
-                if hop > hops:
-                    continue
-                owner = around(chip - hop, chips) if to_right else around(chip + hop, chips)
-                ring(which, None, buffer, owner, hop, to_right).wait_recv()
-                if hop < hops:
-                    one = ring(which, None, buffer, owner, hop + 1, to_right)
-                    one.start()
-                    started.append(one)
-                place = hop if to_right else right_hops + hop
-                one = across(which, None, buffer, owner, place)
-                one.start()
-                started.append(one)
-                expected.append(one)
+        for which in early + late:
+            forward(which, hop)
     for one in expected:
         one.wait_recv()
     for one in started:
@@ -783,64 +803,75 @@
 
 def collect_sums(own, above, slabs, subs):
     chips = subs // 2
+    own_size, above_size = own.shape[0], above.shape[0]
+    chunks = (
+        (0, own_size // 16 * 8),
+        (own_size // 16 * 8, own_size - own_size // 16 * 8),
+        (own_size, above_size // 16 * 8),
+        (own_size + above_size // 16 * 8, above_size - above_size // 16 * 8),
+    )
+    sems = pltpu.SemaphoreType.DMA((len(chunks), chips))
     return pl.pallas_call(
-        functools.partial(collect_kernel, slabs, subs),
-        out_shape=(
-            jax.ShapeDtypeStruct((subs,) + own.shape, jnp.float32),
-            jax.ShapeDtypeStruct((subs,) + above.shape, jnp.float32),
-        ),
+        functools.partial(collect_kernel, slabs, subs, chunks),
+        out_shape=jax.ShapeDtypeStruct((subs, own_size + above_size, LEAF), jnp.float32),
         in_specs=[VMEM, VMEM],
-        out_specs=(VMEM, VMEM),
-        scratch_shapes=[
-            pltpu.SemaphoreType.DMA((3,)),
-            pltpu.SemaphoreType.DMA((2, chips)),
-            pltpu.SemaphoreType.DMA((2, chips)),
-            pltpu.SemaphoreType.DMA((2, chips)),
-            pltpu.SemaphoreType.DMA((2, chips)),
-        ],
+        out_specs=VMEM,
+        scratch_shapes=[pltpu.SemaphoreType.DMA((3,)), sems, sems, sems, sems],
         compiler_params=pltpu.CompilerParams(collective_id=2, has_side_effects=True),
         name="collect_sums",
     )(own, above)
 
 
-def total_kernel(subs, tables, all_own, all_below, out):
-    homes = all_own.shape[1] - 1
+def total_kernel(subs, homes, tables, gathered, out, joined):
+    own_size = packed_rows(homes + 1)
     slab_leaves = subs * homes
 
     def most(k, value):
         return jnp.maximum(value, tables[k, 2 * homes * KINDS])
 
-    shear = lax.fori_loop(0, 4 * subs, most, jnp.int32(0))
+    shear = lax.fori_loop(0, 4 * subs, most, jnp.int32(0), unroll=8)
     shear = jnp.where(lax.axis_index("slab") == 0, shear, 0)
 
-    def one(column, carry):
-        device, place = column // homes, lax.rem(column, homes)
-        mine = all_own[device, place]
-        before = all_own[lax.rem(device + subs - 1, subs), homes]
-        total = mine + jnp.where(place == 0, 1.0, 0.0).astype(jnp.float32) * before
-        source = lax.rem(column - shear + slab_leaves, slab_leaves)
-        device, place = source // homes, lax.rem(source, homes)
-        total = total + all_below[device, place + 1]
-        nearer = all_below[lax.rem(device + subs - 1, subs), homes + 1]
-        later = all_below[lax.rem(device + 1, subs), 0]
-        total = total + jnp.where(place == 0, 1.0, 0.0).astype(jnp.float32) * nearer
-        total = total + jnp.where(place == homes - 1, 1.0, 0.0).astype(jnp.float32) * later
-        start = pl.multiple_of(column * LEAF, LEAF)
-        out[:, pl.ds(start, LEAF)] = total[0:5] * mine[5:6]
+    def part(device, first):
+        return gathered[device, first : first + 5, :]
+
+    def join(device, carry):
+        nearer, later = (device + subs - 1) & (subs - 1), (device + 1) & (subs - 1)
+        for place in range(homes):
+            total = part(device, own_size + 5 * (place + 1))
+            if place == 0:
+                total = total + part(nearer, own_size + 5 * (homes + 1))
+            if place == homes - 1:
+                total = total + part(later, own_size)
+            joined[device * homes + place, 0:5, :] = total
         return carry
 
-    lax.fori_loop(0, slab_leaves, one, 0, unroll=8)
-
-
-def total_rates(tables, all_own, all_below, subs):
-    homes = all_own.shape[1] - 1
+    lax.fori_loop(0, subs, join, 0)
+
+    def add(device, carry):
+        nearer = (device + subs - 1) & (subs - 1)
+        for place in range(homes):
+            total = part(device, 5 * place)
+            if place == 0:
+                total = total + part(nearer, 5 * homes)
+            column = device * homes + place
+            source = (column - shear + slab_leaves) & (slab_leaves - 1)
+            start = pl.multiple_of(column * LEAF, LEAF)
+            out[:, pl.ds(start, LEAF)] = total + joined[source, 0:5, :]
+        return carry
+
+    lax.fori_loop(0, subs, add, 0)
+
+
+def total_rates(tables, gathered, subs, homes):
     return pl.pallas_call(
-        functools.partial(total_kernel, subs),
+        functools.partial(total_kernel, subs, homes),
         out_shape=jax.ShapeDtypeStruct((5, subs * homes * LEAF), jnp.float32),
-        in_specs=[SMEM, VMEM, VMEM],
+        in_specs=[SMEM, VMEM],
         out_specs=VMEM,
+        scratch_shapes=[pltpu.VMEM((subs * homes, 8, LEAF), jnp.float32)],
         name="total_rates",
-    )(tables, all_own, all_below)
+    )(tables, gathered)
 
 
 def shards(slabs, subs, positions, velocity, density, pressure, counts, pair_list):
@@ -859,8 +890,8 @@
     )
     tables = tables.reshape(4 * subs, LEAF)
     own_part, above_part = pair_sums(tables, counts, (below, own, above, beyond), slabs, subs)
-    all_own, all_below = collect_sums(own_part, above_part, slabs, subs)
-    return total_rates(tables, all_own, all_below, subs)
+    gathered = collect_sums(own_part, above_part, slabs, subs)
+    return total_rates(tables, gathered, subs, slab_leaves // subs)
 
 
 def solution(mesh):

time: 111 us -> 106 us (0.955)
  Pallas kernels: 109 us -> 103 us
    pallas_call x1, Pallas kernels: 51 us -> 38.5 us  [pair_sums(): pl.pallas_call(functools.partial(pair_kernel, slabs, subs), out_shape=(ja...]
    pallas_call x2, Pallas kernels: 28.6 us -> 35.3 us  [the longest x1 32.5 us: collect_sums(): pl.pallas_call(functools.partial(collect_kernel, slabs, subs, chunks), ou...]
where the time goes in v4:
time: 106 us; the launch traced here: 105 us
  Pallas kernels  103 us (97%)
    pallas_call x1, Pallas kernels, pair_sums(): pl.pallas_call(functools.partial(pair_kernel, slabs, subs), out_shape=(ja...  38.5 us
    pallas_call x1, Pallas kernels, collect_sums(): pl.pallas_call(functools.partial(collect_kernel, slabs, subs, chunks), ou...  32.5 us
    pallas_call x1, Pallas kernels, exchange(): pl.pallas_call(functools.partial(exchange_kernel, slabs, subs), out_shape...  29.6 us
    pallas_call x1, Pallas kernels, total_rates(): pl.pallas_call(functools.partial(total_kernel, subs, homes), out_shape=ja...  2.74 us

profile of v4, /device:TPU:1, one launch (start us, length us, event | category | flops | bytes accessed | tf_op | source)
XLA Modules:
  0.0 104.8 jit_solution(7261225566956026738)
XLA Ops:
  0.0 0.0 copy-start
  0.0 0.7 copy-done
  0.7 0.1 fusion
  0.8 0.5 add_bitcast_fusion.row_ref
  1.4 29.6 %exchange.1 = (s32[64,1,128]{2,1,0:T(1,128)}, f32[12,8,128]{2,1,0:T(8,128)}, f32[12,8,128]{2,1,0:T(8,128)}, f32[12,8,128]{2,1,0:T(8,128)}, f32[12,8,128]{2,1,0:T(8,128)}) custom-call(s32[1,1,128]{2,1,0:T(1,128)} %add_bitcast_fusion.row_ref, s32[128]{0:T(128)} %counts.3, f32[3,16384]{1,0:T(4,128)} %positions.1, f32[3,16384]{1,0:T(4,128)} %velocity.1, ...), custom_call_target="tpu_custom_call" | custom-call | tf_op jit(solution)/shard_map/exchange/pallas_call | solution.py:190
  31.0 38.5 %pair_sums.1 = (f32[48,128]{1,0:T(8,128)}, f32[56,128]{1,0:T(8,128)}) custom-call(s32[64,128]{1,0:T(8,128)} %bitcast.11, s32[128]{0:T(128)} %counts.3, f32[12,8,128]{2,1,0:T(8,128)} %get-tuple-element.13.below, f32[12,8,128]{2,1,0:T(8,128)} %get-tuple-element.14.own, f32[12,8,128]{2,1,0:T(8,128)} %get-tuple-element.15.above, ...), custom_call_target="tpu_custom_call" | custom-call | tf_op jit(solution)/shard_map/pair_sums/pallas_call | solution.py:663
  69.5 32.5 %collect_sums.1.gathered = f32[16,104,128]{2,1,0:T(8,128)} custom-call(f32[48,128]{1,0:T(8,128)} %get-tuple-element.17.own, f32[56,128]{1,0:T(8,128)} %get-tuple-element.18.above), custom_call_target="tpu_custom_call" | custom-call | tf_op jit(solution)/shard_map/collect_sums/pallas_call | solution.py:814
  102.0 2.7 %total_rates.1 = f32[5,16384]{1,0:T(8,128)} custom-call(s32[64,128]{1,0:T(8,128)} %bitcast.12, f32[16,104,128]{2,1,0:T(8,128)} %collect_sums.1.gathered), custom_call_target="tpu_custom_call" | custom-call | tf_op jit(solution)/shard_map/total_rates/pallas_call | solution.py:867
  (4 shorter events, 0.0 us)
Async XLA Ops:
  0.0 0.7 copy-start

commit v5 on v4

--- a/solution.py
+++ b/solution.py
@@ -25,10 +25,6 @@
 VMEM = pl.BlockSpec(memory_space=pltpu.VMEM)
 SMEM = pl.BlockSpec(memory_space=pltpu.SMEM)
 HIGHEST = lax.Precision.HIGHEST
-
-
-def around(value, size):
-    return lax.rem(value + size, size)
 
 
 def table_row(pair_list, slab, slabs, slab_leaves, homes):
@@ -416,6 +412,9 @@
     planes_two,
     row_sums,
     flux_sums,
+    bases,
+    mine_one,
+    mine_two,
     tiles,
     tile_gaps,
 ):
@@ -465,6 +464,7 @@
     halves = jnp.where((row >= 3) & (row < 6), 0.5, 1.0).astype(jnp.float32)
 
     def finish_one(k, carry):
+        k = jnp.minimum(k, 2 * homes + 2)
         level = jnp.where(k <= homes, 1, 2)
         place = jnp.where(k <= homes, k, k - (homes + 2))
         leaf = level * WIN + place + 2
@@ -521,26 +521,25 @@
             right_parts[leaf, k] = jnp.concatenate([part, pad], axis=0)
         return carry
 
-    lax.fori_loop(0, 2 * homes + 3, finish_one, 0)
+    lax.fori_loop(0, 2 * homes + 4, finish_one, 0, unroll=2)
 
     blank = jnp.zeros((LEAF, LEAF), jnp.float32)
 
-    def turned_left(full, first):
+    def turned_left(full):
         stack = left_stack(full).astype(jnp.float32)
-        parts = ([blank[:first]] if first else []) + [stack, blank[: LEAF - 48 - first]]
-        return jnp.transpose(jnp.concatenate(parts, axis=0)).astype(jnp.bfloat16)
+        return jnp.transpose(jnp.concatenate([stack, blank[:80]], axis=0)).astype(jnp.bfloat16)
 
     def prepare_home(place, carry):
         leaf = own_first + place
         mine = store[leaf] * halves
         for k in range(8):
-            left_parts[place, k] = turned_left(coefficients[leaf, k], 0)
+            left_parts[place, k] = turned_left(coefficients[leaf, k])
         distance = jnp.where(
             row < 3,
             -2.0 * mine,
             jnp.where(row < 6, 0.0, jnp.where(row == 6, length_sq(mine), 1.0)),
         )
-        left_parts[place, 8] = turned_left(distance, 0)
+        left_parts[place, 8] = turned_left(distance)
         turned = jnp.transpose(mine)
         for k in range(5):
             near_rows[place, k] = jnp.broadcast_to(
@@ -575,16 +574,24 @@
         gaps = [tile_gaps[4 * index + k] for k in range(4)]
         return (place, own_first + place, tiles[2 * index + 1], *gaps)
 
-    def lay_planes(index, planes):
+    def ready_tile(index, base_rows, mine_rows):
         place, leaf, other, gap_x, gap_y, gap_v, _ = tile_facts(index)
         theirs = displaced(store[other] * halves, row, gap_x, gap_y, gap_v)
         base = right_stack(flux_base(theirs, row, length_sq(theirs)))
-        base = jnp.concatenate([base, jnp.zeros((16, LEAF), jnp.bfloat16)], axis=0)
+        base_rows[...] = jnp.concatenate([base, jnp.zeros((16, LEAF), jnp.bfloat16)], axis=0)
         mine = store[leaf] * halves - jnp.where(
             row == 0, gap_x, jnp.where(row == 1, gap_y, jnp.where(row == 4, gap_v, 0.0))
         )
-        mine = turned_left(flux_base(mine, row, 0.0), 64)
-        for k in range(8):
+        stack = left_stack(flux_base(mine, row, 0.0)).astype(jnp.float32)
+        mine_rows[...] = jnp.transpose(
+            jnp.concatenate([blank[:64], stack, blank[:16]], axis=0)
+        ).astype(jnp.bfloat16)
+
+    def lay_planes(index, planes, base_rows, mine_rows):
+        place, _, other = tile_facts(index)[:3]
+        base, mine = base_rows[...], mine_rows[...]
+
+        def lay(k):
             right = jnp.concatenate([base, right_parts[other, k]], axis=0)
             left = left_parts[place, k]
             if k < 5:
@@ -601,13 +608,16 @@
                     preferred_element_type=jnp.float32,
                 ).reshape(LEAF // 8, 8, LEAF)
 
+        return lay
+
     def add_fluxes(index, planes, far_rows):
         place, _, other, gap_x, gap_y, gap_v, scale = tile_facts(index)
         theirs = displaced(store[other] * halves, row, gap_x, gap_y, gap_v)
         for k in range(5):
             far_rows[k] = jnp.broadcast_to(theirs[3 + k : 4 + k], (8, LEAF))
         totals = [None] * 5
-        for first in range(0, LEAF // 8, BLOCK):
+
+        def step(first):
             terms = flux_terms(
                 lambda k: planes[k, first : first + BLOCK],
                 lambda k: near_rows[place, k, first : first + BLOCK],
@@ -618,17 +628,44 @@
                 row_sums[place, k, first : first + BLOCK] += terms[k]
                 part = jnp.sum(terms[k], axis=0)
                 totals[k] = part if totals[k] is None else totals[k] + part
-        added = [jnp.sum(part, axis=0, keepdims=True) for part in totals]
-        nothing = jnp.zeros((3, LEAF), jnp.float32)
-        flux_sums[other] = flux_sums[other] + jnp.concatenate(added + [nothing], axis=0)
-
-    lay_planes(0, planes_one)
+
+        def close():
+            added = [jnp.sum(part, axis=0, keepdims=True) for part in totals]
+            nothing = jnp.zeros((3, LEAF), jnp.float32)
+            flux_sums[other] = flux_sums[other] + jnp.concatenate(added + [nothing], axis=0)
+
+        return step, close
+
+    slots = (
+        (planes_one, bases.at[0], mine_one, far_rows.at[0]),
+        (planes_two, bases.at[1], mine_two, far_rows.at[1]),
+    )
+
+    def both(index, this, that):
+        lay = lay_planes(index + 1, *that[:3])
+        step, close = add_fluxes(index, this[0], this[3])
+        steps = list(range(0, LEAF // 8, BLOCK))
+        pace = len(steps) / 8
+        for k in range(8):
+            lay(k)
+            for first in steps[int(k * pace) : int((k + 1) * pace)]:
+                step(first)
+        close()
+        ready_tile(index + 2, *this[1:3])
+
+    ready_tile(0, *slots[0][1:3])
+    ready_tile(1, *slots[1][1:3])
+    first_lay = lay_planes(0, *slots[0][:3])
+    for k in range(8):
+        first_lay(k)
 
     def two_tiles(step, carry):
-        lay_planes(2 * step + 1, planes_two)
-        add_fluxes(2 * step, planes_one, far_rows.at[0])
-        lay_planes(2 * step + 2, planes_one)
-        add_fluxes(2 * step + 1, planes_two, far_rows.at[1])
+        both(2 * step, slots[0], slots[1])
+
+        @pl.when(2 * step + 1 < filled)
+        def _():
+            both(2 * step + 1, slots[1], slots[0])
+
         return carry
 
     lax.fori_loop(0, (filled + 1) // 2, two_tiles, 0)
@@ -643,18 +680,21 @@
         return carry
 
     lax.fori_loop(0, homes, close_home, 0, unroll=2)
-    for out, first, size in (
-        (own_out, own_first, homes + 1),
-        (above_out, above_first, homes + 2),
-    ):
-        out[5 * size :, :] = jnp.zeros((out.shape[0] - 5 * size, LEAF), jnp.float32)
-        for k in range(size):
-            rates = flux_sums[first + k] * numbers[first + k]
-            out[5 * k : 5 * k + 5, :] = rates[0:5]
-
-
-def packed_rows(leaves):
-    return -(-5 * leaves // 8) * 8
+    gap = jnp.zeros((3, LEAF), jnp.float32)
+
+    def put(out, start, leaf, padded):
+        rates = (flux_sums[leaf] * numbers[leaf])[0:5]
+        if padded:
+            out[start : start + 8, :] = jnp.concatenate([rates, gap], axis=0)
+        else:
+            out[start : start + 5, :] = rates
+
+    for k in range(homes):
+        put(own_out, 5 * k, own_first + k, False)
+        put(above_out, 5 * k, above_first + 1 + k, False)
+    put(own_out, 5 * homes, own_first + homes, True)
+    put(above_out, 5 * homes, above_first, True)
+    put(above_out, 5 * homes + 8, above_first + homes + 1, True)
 
 
 def pair_sums(tables, counts, windows, slabs, subs):
@@ -663,8 +703,8 @@
     return pl.pallas_call(
         functools.partial(pair_kernel, slabs, subs),
         out_shape=(
-            jax.ShapeDtypeStruct((packed_rows(homes + 1), LEAF), jnp.float32),
-            jax.ShapeDtypeStruct((packed_rows(homes + 2), LEAF), jnp.float32),
+            jax.ShapeDtypeStruct((5 * homes + 8, LEAF), jnp.float32),
+            jax.ShapeDtypeStruct((5 * homes + 16, LEAF), jnp.float32),
         ),
         in_specs=[SMEM] * 2 + [VMEM] * 4,
         out_specs=(VMEM, VMEM),
@@ -680,6 +720,9 @@
             pltpu.VMEM((PLANES, LEAF // 8, 8, LEAF), jnp.float32),
             pltpu.VMEM((homes, 5, LEAF // 8, 8, LEAF), jnp.float32),
             pltpu.VMEM((leaves, 8, LEAF), jnp.float32),
+            pltpu.VMEM((2, 64, LEAF), jnp.bfloat16),
+            pltpu.VMEM((LEAF, LEAF), jnp.bfloat16),
+            pltpu.VMEM((LEAF, LEAF), jnp.bfloat16),
             pltpu.SMEM((2 * homes * KINDS + 8,), jnp.int32),
             pltpu.SMEM((4 * homes * KINDS + 16,), jnp.float32),
         ],
@@ -688,190 +731,242 @@
 
 
 def collect_kernel(
-    slabs, subs, chunks, own, above, gathered, up_sem, ring_send, ring_recv, core_send, core_recv
+    slabs,
+    subs,
+    own,
+    above,
+    gathered,
+    sheared,
+    got_main,
+    got_edges,
+    near_send,
+    near_recv,
+    chip_send,
+    chip_recv,
+    core_send,
+    core_recv,
+    far_send,
+    far_recv,
+    pass_send,
+    pass_recv,
 ):
     slab = lax.axis_index("slab")
     sub = lax.axis_index("sub")
-    own_size, above_size = own.shape[0], above.shape[0]
+    main = gathered.shape[1]
     chips = subs // 2
-    chip, core = sub // 2, lax.rem(sub, 2)
-    partner = 1 - core
-    ahead, behind = around(chip + 1, chips), around(chip - 1, chips)
-    right_hops = chips // 2
-    left_hops = chips - 1 - right_hops
+    partner = sub + 1 - 2 * (sub & 1)
+    up, down = (slab + 1) & (slabs - 1), (slab - 1 + slabs) & (slabs - 1)
+    after, before = (sub + 1) & (subs - 1), (sub - 1 + subs) & (subs - 1)
+
+    def same_core(k):
+        return (sub + 2 * k + subs) & (subs - 1)
+
     barrier = pltpu.get_barrier_semaphore()
-    for peer in (
-        (around(slab + 1, slabs), sub),
-        (around(slab - 1, slabs), sub),
-        (slab, 2 * ahead + core),
-        (slab, 2 * behind + core),
-        (slab, 2 * chip + partner),
-    ):
+
+    def greet(*peer):
         pl.semaphore_signal(barrier, inc=1, device_id=peer, device_id_type=MESH)
-    pl.semaphore_wait(barrier, 5)
-
-    upward = pltpu.make_async_remote_copy(
-        src_ref=above,
-        dst_ref=gathered.at[sub, pl.ds(own_size, above_size)],
-        send_sem=up_sem.at[0],
-        recv_sem=up_sem.at[1],
-        device_id=(around(slab + 1, slabs), sub),
-        device_id_type=MESH,
-    )
-    upward.start()
-    mine = pltpu.make_async_copy(own, gathered.at[sub, pl.ds(0, own_size)], up_sem.at[2])
-    mine.start()
-
-    def transfer(which, owner_chip, first, peer, send_sem, recv_sem):
-        start, size = chunks[which]
-        target = gathered.at[2 * owner_chip + core, pl.ds(start, size)]
-        source = own.at[pl.ds(start, size)] if first and start < own_size else target
+
+    for peer_slab in (up, down):
+        for peer_sub in (before, sub, after):
+            greet(peer_slab, peer_sub)
+    greet(slab, before)
+    greet(slab, after)
+    for k in range(1, chips):
+        greet(slab, same_core(k))
+    at_seam = (slab == 0) | (slab == slabs - 1)
+
+    @pl.when(at_seam)
+    def _():
+        for k in range(1, chips):
+            greet(slabs - 1 - slab, same_core(k))
+
+    extra = jnp.where(at_seam, chips - 1, 0)
+    pl.semaphore_wait(barrier, 7 + chips + extra)
+
+    def remote(source, target, sems, place, peer):
         return pltpu.make_async_remote_copy(
             src_ref=source,
             dst_ref=target,
-            send_sem=send_sem,
-            recv_sem=recv_sem,
-            device_id=(slab, peer),
+            send_sem=sems[0].at[place],
+            recv_sem=sems[1].at[place],
+            device_id=peer,
             device_id_type=MESH,
         )
 
-    def ring(which, owner_chip, hop, to_right):
-        place = (hop - 1) if to_right else (right_hops + hop - 1)
-        return transfer(
-            which,
-            owner_chip,
-            hop == 1,
-            2 * (ahead if to_right else behind) + core,
-            ring_send.at[which, place],
-            ring_recv.at[which, place],
-        )
-
-    def across(which, owner_chip, place):
-        return transfer(
-            which,
-            owner_chip,
-            place == 0,
-            2 * chip + partner,
-            core_send.at[which, place],
-            core_recv.at[which, place],
-        )
-
-    started, expected = [], []
-
-    def launch(which):
-        for to_right, hops in ((True, right_hops), (False, left_hops)):
-            if hops > 0:
-                one = ring(which, chip, 1, to_right)
-                one.start()
-                started.append(one)
-        one = across(which, chip, 0)
-        one.start()
-        started.append(one)
-        expected.append(one)
-
-    def forward(which, hop):
-        for to_right, hops in ((True, right_hops), (False, left_hops)):
-            if hop > hops:
-                continue
-            owner = around(chip - hop, chips) if to_right else around(chip + hop, chips)
-            ring(which, owner, hop, to_right).wait_recv()
-            if hop < hops:
-                one = ring(which, owner, hop + 1, to_right)
-                one.start()
-                started.append(one)
-            one = across(which, owner, hop if to_right else right_hops + hop)
+    near = (near_send, near_recv)
+    edge = pl.ds(main, 8)
+    last_edge = pl.ds(main + 8, 8)
+    right = remote(own.at[edge], got_edges.at[0], near, 0, (slab, after))
+    right.start()
+    upward = (
+        remote(above.at[pl.ds(0, main)], got_main, near, 1, (up, sub)),
+        remote(above.at[edge], got_edges.at[1], near, 2, (up, before)),
+        remote(above.at[last_edge], got_edges.at[2], near, 3, (up, after)),
+    )
+
+    def far(k):
+        return remote(above, sheared.at[sub], (far_send, far_recv), k, (up, same_core(k)))
+
+    def far_arrival(k):
+        return remote(
+            above, sheared.at[same_core(-k)], (far_send, far_recv), k, (up, same_core(k))
+        )
+
+    @pl.when(slab != slabs - 1)
+    def _():
+        for one in upward:
             one.start()
-            started.append(one)
-            expected.append(one)
-
-    early = [k for k, (start, _) in enumerate(chunks) if start < own_size]
-    late = [k for k, (start, _) in enumerate(chunks) if start >= own_size]
-    for which in early:
-        launch(which)
-    upward.wait()
-    for which in late:
-        launch(which)
-    mine.wait()
-    for hop in range(1, right_hops + 1):
-        for which in early + late:
-            forward(which, hop)
-    for one in expected:
-        one.wait_recv()
-    for one in started:
-        one.wait_send()
+
+    @pl.when(slab == slabs - 1)
+    def _():
+        for k in range(chips):
+            far(k).start()
+
+    right.wait_recv()
+
+    @pl.when(slab != 0)
+    def _():
+        for one in upward:
+            one.wait_recv()
+        gathered[sub] = own[0:main] + got_main[...]
+        gathered[sub, 0:5] = gathered[sub, 0:5] + (got_edges[0, 0:5] + got_edges[2, 0:5])
+        gathered[sub, main - 5 : main] = gathered[sub, main - 5 : main] + got_edges[1, 0:5]
+
+    @pl.when(slab == 0)
+    def _():
+        gathered[sub] = own[0:main]
+        gathered[sub, 0:5] = gathered[sub, 0:5] + got_edges[0, 0:5]
+
+    def to_chip(k, slot):
+        return remote(
+            gathered.at[sub],
+            gathered.at[slot],
+            (chip_send, chip_recv),
+            k,
+            (slab, same_core(k)),
+        )
+
+    def to_core(k):
+        block = gathered.at[same_core(-k)]
+        return remote(block, block, (core_send, core_recv), k, (slab, partner))
+
+    def pass_on(k):
+        block = sheared.at[same_core(-k)]
+        return remote(block, block, (pass_send, pass_recv), k, (slab, partner))
+
+    order = sorted(range(1, chips), key=lambda k: -min(k, chips - k))
+    for k in order:
+        to_chip(k, sub).start()
+    to_core(0).start()
+    for k in reversed(order):
+        to_chip(k, same_core(-k)).wait_recv()
+        to_core(k).start()
+
+    @pl.when(slab == 0)
+    def _():
+        for k in [0] + order[::-1]:
+            far_arrival(k).wait_recv()
+            pass_on(k).start()
+        for k in range(chips):
+            pass_on(k).wait_recv()
+            pass_on(k).wait_send()
+
+    for k in range(chips):
+        to_core(k).wait_recv()
+        to_core(k).wait_send()
+    for k in order:
+        to_chip(k, sub).wait_send()
+    right.wait_send()
+
+    @pl.when(slab != slabs - 1)
+    def _():
+        for one in upward:
+            one.wait_send()
+
+    @pl.when(slab == slabs - 1)
+    def _():
+        for k in range(chips):
+            far(k).wait_send()
 
 
 def collect_sums(own, above, slabs, subs):
     chips = subs // 2
-    own_size, above_size = own.shape[0], above.shape[0]
-    chunks = (
-        (0, own_size // 16 * 8),
-        (own_size // 16 * 8, own_size - own_size // 16 * 8),
-        (own_size, above_size // 16 * 8),
-        (own_size + above_size // 16 * 8, above_size - above_size // 16 * 8),
-    )
-    sems = pltpu.SemaphoreType.DMA((len(chunks), chips))
+    main = own.shape[0] - 8
     return pl.pallas_call(
-        functools.partial(collect_kernel, slabs, subs, chunks),
-        out_shape=jax.ShapeDtypeStruct((subs, own_size + above_size, LEAF), jnp.float32),
+        functools.partial(collect_kernel, slabs, subs),
+        out_shape=(
+            jax.ShapeDtypeStruct((subs, main, LEAF), jnp.float32),
+            jax.ShapeDtypeStruct((subs, main + 16, LEAF), jnp.float32),
+        ),
         in_specs=[VMEM, VMEM],
-        out_specs=VMEM,
-        scratch_shapes=[pltpu.SemaphoreType.DMA((3,)), sems, sems, sems, sems],
+        out_specs=(VMEM, VMEM),
+        scratch_shapes=[
+            pltpu.VMEM((main, LEAF), jnp.float32),
+            pltpu.VMEM((3, 8, LEAF), jnp.float32),
+            pltpu.SemaphoreType.DMA((4,)),
+            pltpu.SemaphoreType.DMA((4,)),
+        ]
+        + [pltpu.SemaphoreType.DMA((chips,))] * 8,
         compiler_params=pltpu.CompilerParams(collective_id=2, has_side_effects=True),
         name="collect_sums",
     )(own, above)
 
 
-def total_kernel(subs, homes, tables, gathered, out, joined):
-    own_size = packed_rows(homes + 1)
+def total_kernel(subs, homes, tables, gathered, sheared, out, joined):
     slab_leaves = subs * homes
-
-    def most(k, value):
-        return jnp.maximum(value, tables[k, 2 * homes * KINDS])
-
-    shear = lax.fori_loop(0, 4 * subs, most, jnp.int32(0), unroll=8)
-    shear = jnp.where(lax.axis_index("slab") == 0, shear, 0)
-
-    def part(device, first):
-        return gathered[device, first : first + 5, :]
-
-    def join(device, carry):
-        nearer, later = (device + subs - 1) & (subs - 1), (device + 1) & (subs - 1)
-        for place in range(homes):
-            total = part(device, own_size + 5 * (place + 1))
-            if place == 0:
-                total = total + part(nearer, own_size + 5 * (homes + 1))
-            if place == homes - 1:
-                total = total + part(later, own_size)
-            joined[device * homes + place, 0:5, :] = total
-        return carry
-
-    lax.fori_loop(0, subs, join, 0)
-
-    def add(device, carry):
-        nearer = (device + subs - 1) & (subs - 1)
-        for place in range(homes):
-            total = part(device, 5 * place)
-            if place == 0:
-                total = total + part(nearer, 5 * homes)
-            column = device * homes + place
-            source = (column - shear + slab_leaves) & (slab_leaves - 1)
-            start = pl.multiple_of(column * LEAF, LEAF)
-            out[:, pl.ds(start, LEAF)] = total + joined[source, 0:5, :]
-        return carry
-
-    lax.fori_loop(0, subs, add, 0)
-
-
-def total_rates(tables, gathered, subs, homes):
+    main = 5 * homes
+    first_slab = lax.axis_index("slab") == 0
+
+    def place_all(extra):
+        def one(device, carry):
+            for place in range(homes):
+                column = device * homes + place
+                start = pl.multiple_of(column * LEAF, LEAF)
+                total = gathered[device, 5 * place : 5 * place + 5, :]
+                if extra is not None:
+                    total = total + extra(column)
+                out[:, pl.ds(start, LEAF)] = total
+            return carry
+
+        lax.fori_loop(0, subs, one, 0)
+
+    @pl.when(jnp.logical_not(first_slab))
+    def _():
+        place_all(None)
+
+    @pl.when(first_slab)
+    def _():
+        def most(k, value):
+            return jnp.maximum(value, tables[k, 2 * homes * KINDS])
+
+        shear = lax.fori_loop(0, 4 * subs, most, jnp.int32(0), unroll=8)
+
+        def join(device, carry):
+            nearer, later = (device + subs - 1) & (subs - 1), (device + 1) & (subs - 1)
+            for place in range(homes):
+                total = sheared[device, 5 * place : 5 * place + 5, :]
+                if place == 0:
+                    total = total + sheared[nearer, main + 8 : main + 13, :]
+                if place == homes - 1:
+                    total = total + sheared[later, main : main + 5, :]
+                joined[device * homes + place, 0:5, :] = total
+            return carry
+
+        lax.fori_loop(0, subs, join, 0)
+        place_all(
+            lambda column: joined[(column - shear + slab_leaves) & (slab_leaves - 1), 0:5, :]
+        )
+
+
+def total_rates(tables, gathered, sheared, subs, homes):
     return pl.pallas_call(
         functools.partial(total_kernel, subs, homes),
         out_shape=jax.ShapeDtypeStruct((5, subs * homes * LEAF), jnp.float32),
-        in_specs=[SMEM, VMEM],
+        in_specs=[SMEM, VMEM, VMEM],
         out_specs=VMEM,
         scratch_shapes=[pltpu.VMEM((subs * homes, 8, LEAF), jnp.float32)],
         name="total_rates",
-    )(tables, gathered)
+    )(tables, gathered, sheared)
 
 
 def shards(slabs, subs, positions, velocity, density, pressure, counts, pair_list):
@@ -890,8 +985,8 @@
     )
     tables = tables.reshape(4 * subs, LEAF)
     own_part, above_part = pair_sums(tables, counts, (below, own, above, beyond), slabs, subs)
-    gathered = collect_sums(own_part, above_part, slabs, subs)
-    return total_rates(tables, gathered, subs, slab_leaves // subs)
+    gathered, sheared = collect_sums(own_part, above_part, slabs, subs)
+    return total_rates(tables, gathered, sheared, subs, slab_leaves // subs)
 
 
 def solution(mesh):

time: 106 us -> 97.8 us (0.923); the launches traced: 105 us -> 97.8 us
  Pallas kernels: 103 us -> 96.4 us
    pallas_call x1, Pallas kernels: 38.5 us -> 33.4 us  [pair_sums(): pl.pallas_call(functools.partial(pair_kernel, slabs, subs), out_shape=(ja...]
    pallas_call x1, Pallas kernels: 32.5 us -> 30.6 us  [collect_sums(): pl.pallas_call(functools.partial(collect_kernel, slabs, subs), out_shape=...]
where the time goes in v5:
time: 97.8 us
  Pallas kernels  96.4 us (99%)
    pallas_call x1, Pallas kernels, pair_sums(): pl.pallas_call(functools.partial(pair_kernel, slabs, subs), out_shape=(ja...  33.4 us
    pallas_call x1, Pallas kernels, collect_sums(): pl.pallas_call(functools.partial(collect_kernel, slabs, subs), out_shape=...  30.6 us
    pallas_call x1, Pallas kernels, exchange(): pl.pallas_call(functools.partial(exchange_kernel, slabs, subs), out_shape...  29.6 us
    pallas_call x1, Pallas kernels, total_rates(): pl.pallas_call(functools.partial(total_kernel, subs, homes), out_shape=ja...  2.71 us

profile of v5, /device:TPU:1, one launch (start us, length us, event | category | flops | bytes accessed | tf_op | source)
XLA Modules:
  0.0 97.8 jit_solution(10083178741490366806)
XLA Ops:
  0.0 0.0 copy-start
  0.0 0.7 copy-done
  0.7 0.1 fusion
  0.8 0.5 add_bitcast_fusion.row_ref
  1.4 29.6 %exchange.1 = (s32[64,1,128]{2,1,0:T(1,128)}, f32[12,8,128]{2,1,0:T(8,128)}, f32[12,8,128]{2,1,0:T(8,128)}, f32[12,8,128]{2,1,0:T(8,128)}, f32[12,8,128]{2,1,0:T(8,128)}) custom-call(s32[1,1,128]{2,1,0:T(1,128)} %add_bitcast_fusion.row_ref, s32[128]{0:T(128)} %counts.3, f32[3,16384]{1,0:T(4,128)} %positions.1, f32[3,16384]{1,0:T(4,128)} %velocity.1, ...), custom_call_target="tpu_custom_call" | custom-call | tf_op jit(solution)/shard_map/exchange/pallas_call | solution.py:186
  31.0 33.4 %pair_sums.1 = (f32[48,128]{1,0:T(8,128)}, f32[56,128]{1,0:T(8,128)}) custom-call(s32[64,128]{1,0:T(8,128)} %bitcast.11, s32[128]{0:T(128)} %counts.3, f32[12,8,128]{2,1,0:T(8,128)} %get-tuple-element.15.below, f32[12,8,128]{2,1,0:T(8,128)} %get-tuple-element.16.own, f32[12,8,128]{2,1,0:T(8,128)} %get-tuple-element.17.above, ...), custom_call_target="tpu_custom_call" | custom-call | tf_op jit(solution)/shard_map/pair_sums/pallas_call | solution.py:703
  64.4 30.6 %collect_sums.1 = (f32[16,40,128]{2,1,0:T(8,128)}, f32[16,56,128]{2,1,0:T(8,128)}) custom-call(f32[48,128]{1,0:T(8,128)} %get-tuple-element.19.own, f32[56,128]{1,0:T(8,128)} %get-tuple-element.20.above), custom_call_target="tpu_custom_call" | custom-call | tf_op jit(solution)/shard_map/collect_sums/pallas_call | solution.py:895
  95.1 2.7 %total_rates.1 = f32[5,16384]{1,0:T(8,128)} custom-call(s32[64,128]{1,0:T(8,128)} %bitcast.12, f32[16,40,128]{2,1,0:T(8,128)} %get-tuple-element.21.gathered, f32[16,56,128]{2,1,0:T(8,128)} %get-tuple-element.22.sheared), custom_call_target="tpu_custom_call" | custom-call | tf_op jit(solution)/shard_map/total_rates/pallas_call | solution.py:962
  (4 shorter events, 0.0 us)
Async XLA Ops:
  0.0 0.7 copy-start
